TPU v7x, 32 devices: a whole 2x2x4 slice. The times are simulated.
32 devices in a mesh: group: 2 (over x), wide: 16 (over z, y, core).
Axes of the slice: x: 2, y: 2, z: 4, core: 2. Of those that a mesh axis runs over, the one named last changes fastest.
Arguments:
- stream_index: int32 [2], P('group'), parts along dimension 0, may hold values from 0 to 16777215
- forcing: bfloat16 [32, 1536, 1536], P('group', 'wide'), parts along dimension 0, may hold values from -144 to 144
Outputs:
- pressure: bfloat16 [32, 1536, 1536], P('group', 'wide'), parts along dimension 0
There are 2 independent parts, one for each index of `group`. A program takes and returns all parts, laid end to end along the dimension named above; each array names one. Nothing has to cross between parts.
All inputs are finite; a program needn't handle non-finite values.
Results may differ from a plain program's by a relative error of at most 0.0045.
Values may be sent and summed in bfloat16 or wider, within the bound.
No kernel may reach another device: no remote copies, remote signals or barrier semaphores. Data moves between devices by JAX's collectives and lax.ppermute only.
A program may use at most 192 MiB of HBM per device.

v0:
```python
import math

import jax
import jax.numpy as jnp
from jax import lax
from jax.sharding import PartitionSpec as P

LEN_X = 1536
LEN_Y = 1536
ITERS = 4


def with_halo(block, sides, width):
    for axis, dim in sides:
        count = lax.axis_size(axis)
        forward = [(i, i + 1) for i in range(count - 1)]
        backward = [(target, source) for source, target in forward]
        low = lax.ppermute(
            lax.slice_in_dim(block, block.shape[dim] - width, None, axis=dim), axis, forward
        )
        high = lax.ppermute(lax.slice_in_dim(block, 0, width, axis=dim), axis, backward)
        block = jnp.concatenate([low, block, high], axis=dim)
    return block


def scramble(value):
    value = value ^ value >> 16 & 65535
    value = value * 73244475
    value = value ^ value >> 16 & 65535
    value = value * 73244475
    value = value ^ value >> 16 & 65535
    return value


def cosine_basis(length):
    row_idx = lax.broadcasted_iota(jnp.int32, (length, length), 0)
    mode_idx = lax.broadcasted_iota(jnp.int32, (length, length), 1)
    phase = (2 * row_idx + 1) * mode_idx % (4 * length)
    angle = phase.astype(jnp.float32) * (math.pi / (2.0 * length))
    weights = jnp.where(mode_idx == 0, math.sqrt(1.0 / length), math.sqrt(2.0 / length))
    return (weights * jnp.cos(angle)).astype(jnp.bfloat16)


def coefficient_plane(stream_key, mode_z, depth):
    mode_x = lax.broadcasted_iota(jnp.int32, (LEN_X, LEN_Y), 0)
    mode_y = lax.broadcasted_iota(jnp.int32, (LEN_X, LEN_Y), 1)
    counter = (mode_z * LEN_X + mode_x) * LEN_Y + mode_y
    bits_a = scramble(2 * counter ^ stream_key)
    bits_b = scramble(2 * counter + 1 ^ stream_key)
    uniform_a = (bits_a >> 8 & 16777215).astype(jnp.float32) * 2.0 ** (-24) + 2.0 ** (-25)
    uniform_b = (bits_b >> 8 & 16777215).astype(jnp.float32) * 2.0 ** (-24) + 2.0 ** (-25)
    noise = jnp.sqrt(-2.0 * jnp.log(uniform_a)) * jnp.cos(2.0 * math.pi * uniform_b)
    freq_x = mode_x.astype(jnp.float32) * (math.pi / LEN_X)
    freq_y = mode_y.astype(jnp.float32) * (math.pi / LEN_Y)
    freq_z = mode_z.astype(jnp.float32) * (math.pi / depth)
    amplitude = 1.0 / jnp.sqrt(0.05 + freq_x * freq_x + freq_y * freq_y + freq_z * freq_z)
    return (amplitude * noise).astype(jnp.bfloat16)


def contract_last(left, table):
    return lax.dot_general(
        left, table, (((left.ndim - 1,), (1,)), ((), ())), preferred_element_type=jnp.float32
    )


def operate(wide_p, wide_k):
    center_p = wide_p[:, 1:-1]
    center_k = wide_k[:, 1:-1]
    total = 0.5 * (center_k + wide_k[:, 2:]) * (center_p - wide_p[:, 2:])
    total = total + 0.5 * (center_k + wide_k[:, :-2]) * (center_p - wide_p[:, :-2])
    for axis in (0, 2):
        widths = [(0, 0), (0, 0), (0, 0)]
        widths[axis] = (1, 1)
        padded_p = jnp.pad(center_p, widths)
        padded_k = jnp.pad(center_k, widths)
        size_here = center_p.shape[axis]
        for start in (0, 2):
            near_p = lax.slice_in_dim(padded_p, start, start + size_here, axis=axis)
            near_k = lax.slice_in_dim(padded_k, start, start + size_here, axis=axis)
            total = total + 0.5 * (center_k + near_k) * (center_p - near_p)
    return total


def body(stream_index, forcing):
    depth = forcing.shape[0]
    planes_here = depth // lax.axis_size("wide")
    stream_key = scramble(stream_index[0] ^ 1540483477)
    basis_x = cosine_basis(LEN_X)
    basis_y = cosine_basis(LEN_Y)
    basis_z = cosine_basis(depth)
    first_mode = lax.axis_index("wide") * planes_here
    own_modes = first_mode + jnp.arange(planes_here, dtype=jnp.int32)

    def rows_for(mode_z):
        coeff = coefficient_plane(stream_key, mode_z, depth)
        return jnp.dot(basis_x, coeff, preferred_element_type=jnp.float32).astype(jnp.bfloat16)

    def both_axes(mode_z):
        return contract_last(rows_for(mode_z), basis_y).astype(jnp.bfloat16)

    planes = lax.map(both_axes, own_modes)
    block = lax.all_to_all(planes, "wide", split_axis=1, concat_axis=0, tiled=True)
    count_z, count_x, count_y = block.shape
    field = jnp.dot(
        basis_z, block.reshape(count_z, count_x * count_y), preferred_element_type=jnp.float32
    )
    field = field.reshape(count_z, count_x, count_y)
    perm = jnp.exp(1.5 * jnp.tanh(2.0 * field))
    source = forcing.astype(jnp.float32)
    theta = 27.9
    delta = 26.1
    sigma = theta / delta
    rho = 1.0 / sigma
    step = source / theta
    press = step
    perm_wide = with_halo(perm.astype(jnp.bfloat16), (("wide", 1),), 1).astype(perm.dtype)
    for count in range(ITERS - 1):
        press_wide = with_halo(press, (("wide", 1),), 1)
        resid = source - operate(press_wide, perm_wide)
        rho_next = 1.0 / (2.0 * sigma - rho)
        step = rho_next * rho * step + 2.0 * rho_next / delta * resid
        press = press + step
        rho = rho_next
    return press.astype(jnp.bfloat16)


def solution(mesh):
    return jax.shard_map(
        body,
        mesh=mesh,
        in_specs=(P("group"), P("group", "wide", None)),
        out_specs=P("group", "wide", None),
        check_vma=False,
    )
```

profile of v0, /device:TPU:18, one launch (start us, length us, event | category | flops | bytes accessed | tf_op | source)
XLA Modules:
  0.0 644.6 jit_solution(15394397886811121742)
XLA Ops:
  0.7 36.9 %fusion.145 = bf16[1536,1536]{1,0:T(8,128)(2,1)S(1)} fusion(s32[1536]{0:T(1024)S(1)} %get-tuple-element.48, f32[1536]{0:T(1024)S(1)} %get-tuple-element.50), kind=kLoop, calls=%fused_computation.60.clone.clone.1 | loop fusion | flops 25952256 | bytes 4730880 | tf_op jit(solution)/shard_map/while/body/eval_jaxpr/dot_general | solution.py:61
  37.6 45.8 %multiply_convert_fusion.5 = bf16[1536,1536]{1,0:T(8,128)(2,1)S(1)} fusion(s32[]{:T(128)S(6)} %xor.65, s32[1536]{0:T(1024)S(1)} %get-tuple-element.47, f32[]{:T(128)S(6)} %mul.293, f32[1536]{0:T(1024)S(1)} %get-tuple-element.49, f32[1536]{0:T(1024)S(1)} %broadcast_add_fusion), kind=kLoop, calls=%fused_computation.101.clone.clone.2 | loop fusion | flops 103809024 | bytes 4737032 | tf_op jit(solution)/shard_map/while/body/eval_jaxpr/dot_general | solution.py:96
  83.4 42.6 %convolution_convert_fusion.1 = bf16[1536,1536]{1,0:T(8,128)(2,1)S(1)} fusion(s32[1536]{0:T(1024)S(1)} %get-tuple-element.48, f32[1536]{0:T(1024)S(1)} %get-tuple-element.50, bf16[1536,1536]{1,0:T(8,128)(2,1)S(1)} %multiply_convert_fusion.5), kind=kOutput, calls=%fused_computation.107 | convolution fusion | flops 7276068864 | bytes 9449472 | tf_op jit(solution)/shard_map/while/body/eval_jaxpr/dot_general | solution.py:96
  126.1 7.9 %fusion.71 = bf16[1,1536,1536]{2,1,0:T(8,128)(2,1)S(1)} fusion(bf16[1536,1536]{1,0:T(8,128)(2,1)S(1)} %convolution_convert_fusion.1, bf16[1536,1536]{1,0:T(8,128)(2,1)S(1)} %fusion.145), kind=kOutput, calls=%fused_computation.108 | convolution fusion | flops 7250116608 | bytes 14155776 | tf_op jit(solution)/shard_map/while/body/eval_jaxpr/dot_general | solution.py:61
  134.0 52.2 %copy.30 = bf16[1,1536,1536]{2,0,1:T(2,128)(2,1)} copy(bf16[1,1536,1536]{2,1,0:T(8,128)(2,1)S(1)} %fusion.71) | data formatting | bytes 9437184 | tf_op jit(solution)/shard_map/while/body/jit(dynamic_update_index_in_dim)/broadcast_in_dim | solution.py:101
  186.8 31.9 %reduce.2 = bf16[1536,1536]{1,0:T(8,128)(2,1)} reduce(bf16[1536,1,1536]{2,1,0:T(2,128)(2,1)} %bitcast.21, bf16[]{:T(256)} %broadcast.337), dimensions={1}, to_apply=%bitcast.20.reduce_sub_computation | reduce | bytes 9437186
  218.7 11.8 %reshape.15 = bf16[16,2,73728]{2,1,0:T(2,128)(2,1)} reshape(bf16[1536,1536]{1,0:T(8,128)(2,1)} %reduce.2) | data formatting | bytes 9437184
  230.5 6.5 %all-to-all-start = ((bf16[16,2,73728]{2,1,0:T(2,128)(2,1)}), bf16[16,2,73728]{2,1,0:T(2,128)(2,1)}, u32[]{:S(2)}, u32[]{:S(2)}) async-start(bf16[16,2,73728]{2,1,0:T(2,128)(2,1)} %reshape.15), calls=%async_computation | async-start | bytes 9437184 | tf_op jit(solution)/shard_map/all_to_all | solution.py:102
  237.1 9.6 %convert_multiply_fusion.1 = f32[16,96,1536]{2,0,1:T(8,128)} fusion(bf16[16,96,1536]{2,1,0:T(8,128)(2,1)} %param.3), kind=kLoop, calls=%fused_computation.4 | loop fusion | flops 4718592 | bytes 14155776 | tf_op jit(solution)/shard_map/div | solution.py:114
  246.7 94.1 %all-to-all-done = bf16[16,2,73728]{2,1,0:T(2,128)(2,1)} async-done(((bf16[16,2,73728]{2,1,0:T(2,128)(2,1)}), bf16[16,2,73728]{2,1,0:T(2,128)(2,1)}, u32[]{:S(2)}, u32[]{:S(2)}) %all-to-all-start) | async-done | bytes 4718624 | tf_op jit(solution)/shard_map/all_to_all | solution.py:102
  340.8 12.8 %reshape.16 = bf16[1536,1,1536]{2,1,0:T(2,128)(2,1)} reshape(bf16[16,2,73728]{2,1,0:T(2,128)(2,1)} %all-to-all-done) | data formatting | bytes 9437184
  353.6 31.3 %bitcast_reduce_fusion = bf16[1536,1536]{1,0:T(8,128)(2,1)} fusion(bf16[1536,1,1536]{2,1,0:T(2,128)(2,1)} %reshape.16), kind=kLoop, calls=%fused_computation.181 | loop fusion | bytes 9437184 | tf_op jit(solution)/shard_map/all_to_all | solution.py:102
  385.0 5.2 reshape.12
  390.2 5.1 exponential_convert_fusion
  397.2 4.5 collective-permute-start.1
  408.1 5.0 slice.154
  414.9 59.3 %fusion = (f32[16,96,1536]{2,0,1:T(8,128)}, f32[16,96,1536]{2,0,1:T(8,128)}) fusion(bf16[16,96,1536]{2,1,0:T(8,128)(2,1)} %param.3, f32[16,96,1536]{2,0,1:T(8,128)} %slice.154, f32[16,96,1536]{2,0,1:T(8,128)} %convert_multiply_fusion.1, f32[16,1,1536]{2,0,1:T(8,128)S(1)} %collective-permute-done.3, f32[16,98,1536]{2,0,1:T(8,128)} %copy-done, ...), kind=kLoop, calls=%fused_computation.14 | loop fusion | flops 89653248 | bytes 70975488 | tf_op jit(solution)/shard_map/add | solution.py:122
  475.2 4.1 collective-permute-start.4
  481.4 4.6 collective-permute-done.5
  486.1 69.9 %fusion.92 = (f32[16,96,1536]{2,0,1:T(8,128)}, f32[16,96,1536]{2,0,1:T(8,128)}) fusion(f32[16,96,1536]{2,0,1:T(8,128)} %get-tuple-element.38, bf16[16,96,1536]{2,1,0:T(8,128)(2,1)} %param.3, f32[16,96,1536]{2,0,1:T(8,128)} %get-tuple-element.37, f32[16,96,1536]{2,0,1:T(8,128)} %slice.154, f32[16,1,1536]{2,0,1:T(8,128)S(1)} %collective-permute-done.5, ...), kind=kLoop, calls=%fused_computation.128 | loop fusion | flops 92012544 | bytes 80412672 | tf_op jit(solution)/shard_map/add | solution.py:122
  558.8 2.7 collective-permute-start.7
  561.5 4.1 collective-permute-done.7
  565.7 71.4 %add_convert_fusion = bf16[16,96,1536]{2,0,1:T(8,128)(2,1)} fusion(f32[16,96,1536]{2,0,1:T(8,128)} %get-tuple-element.35, f32[16,96,1536]{2,0,1:T(8,128)} %get-tuple-element.36, f32[16,1,1536]{2,0,1:T(8,128)S(1)} %collective-permute-done.7, f32[16,1,1536]{2,0,1:T(8,128)S(1)} %collective-permute-done.6, bf16[16,96,1536]{2,1,0:T(8,128)(2,1)} %param.3, ...), kind=kLoop, calls=%fused_computation.98 | loop fusion | flops 89653248 | bytes 66256896 | tf_op jit(solution)/shard_map/convert_element_type | solution.py:124
  637.0 7.1 %copy.15 = bf16[16,96,1536]{2,1,0:T(8,128)(2,1)} copy(bf16[16,96,1536]{2,0,1:T(8,128)(2,1)} %add_convert_fusion) | data formatting | bytes 9437184 | tf_op jit(solution)/shard_map/convert_element_type | solution.py:124
  (24 shorter events, 16.6 us)
Async XLA Ops:
  230.5 110.3 %all-to-all-start = ((bf16[16,2,73728]{2,1,0:T(2,128)(2,1)}), bf16[16,2,73728]{2,1,0:T(2,128)(2,1)}, u32[]{:S(2)}, u32[]{:S(2)}) async-start(bf16[16,2,73728]{2,1,0:T(2,128)(2,1)} %reshape.15), calls=%async_computation | async-start | bytes 9437184 | tf_op jit(solution)/shard_map/all_to_all | solution.py:102
  395.3 12.0 %collective-permute-start = (bf16[16,1,1536]{2,0,1:T(8,128)(2,1)S(1)}, bf16[16,1,1536]{2,0,1:T(8,128)(2,1)S(1)}, u32[]{:S(2)}, u32[]{:S(2)}) collective-permute-start(bf16[16,1,1536]{2,0,1:T(8,128)(2,1)S(1)} %get-tuple-element.45), channel_id=1, source_target_pairs={{0,1},{1,2},{2,3},{3,4},{4,5},{5,6},{6,7},{7,8},{8,9},{9,10},{10,1... | collective-permute-start | bytes 147464 | tf_op jit(solution)/shard_map/ppermute | solution.py:18
  397.2 10.1 %collective-permute-start.1 = (bf16[16,1,1536]{2,0,1:T(8,128)(2,1)S(1)}, bf16[16,1,1536]{2,0,1:T(8,128)(2,1)S(1)}, u32[]{:S(2)}, u32[]{:S(2)}) collective-permute-start(bf16[16,1,1536]{2,0,1:T(8,128)(2,1)S(1)} %get-tuple-element.46), channel_id=1, source_target_pairs={{1,0},{2,1},{3,2},{4,3},{5,4},{6,5},{7,6},{8,7},{9,8},{10,9},{11,1... | collective-permute-start | bytes 147464 | tf_op jit(solution)/shard_map/ppermute | solution.py:21
  402.7 12.2 %collective-permute-start.2 = (f32[16,1,1536]{2,0,1:T(8,128)S(1)}, f32[16,1,1536]{2,0,1:T(8,128)S(1)}, u32[]{:S(2)}, u32[]{:S(2)}) collective-permute-start(f32[16,1,1536]{2,0,1:T(8,128)S(1)} %get-tuple-element.43), channel_id=1, source_target_pairs={{1,0},{2,1},{3,2},{4,3},{5,4},{6,5},{7,6},{8,7},{9,8},{10,9},{11,1... | collective-permute-start | bytes 294920 | tf_op jit(solution)/shard_map/ppermute | solution.py:21
  404.6 10.2 %collective-permute-start.3 = (f32[16,1,1536]{2,0,1:T(8,128)S(1)}, f32[16,1,1536]{2,0,1:T(8,128)S(1)}, u32[]{:S(2)}, u32[]{:S(2)}) collective-permute-start(f32[16,1,1536]{2,0,1:T(8,128)S(1)} %get-tuple-element.44), channel_id=1, source_target_pairs={{0,1},{1,2},{2,3},{3,4},{4,5},{5,6},{6,7},{7,8},{8,9},{9,10},{10,1... | collective-permute-start | bytes 294920 | tf_op jit(solution)/shard_map/ppermute | solution.py:18
  408.1 6.8 %copy-start = (f32[16,98,1536]{2,0,1:T(8,128)}, f32[16,98,1536]{2,0,1:T(8,128)S(1)}, u32[]{:S(2)}) copy-start(f32[16,98,1536]{2,0,1:T(8,128)S(1)} %maximum_convert_fusion) | copy-start | bytes 28901380
  475.2 6.3 collective-permute-start.4
  479.2 6.8 %collective-permute-start.5 = (f32[16,1,1536]{2,0,1:T(8,128)S(1)}, f32[16,1,1536]{2,0,1:T(8,128)S(1)}, u32[]{:S(2)}, u32[]{:S(2)}) collective-permute-start(f32[16,1,1536]{2,0,1:T(8,128)S(1)} %get-tuple-element.42), channel_id=1, source_target_pairs={{0,1},{1,2},{2,3},{3,4},{4,5},{5,6},{6,7},{7,8},{8,9},{9,10},{10,1... | collective-permute-start | bytes 294920 | tf_op jit(solution)/shard_map/ppermute | solution.py:18
  556.9 4.6 collective-permute-start.6
  558.8 6.8 %collective-permute-start.7 = (f32[16,1,1536]{2,0,1:T(8,128)S(1)}, f32[16,1,1536]{2,0,1:T(8,128)S(1)}, u32[]{:S(2)}, u32[]{:S(2)}) collective-permute-start(f32[16,1,1536]{2,0,1:T(8,128)S(1)} %get-tuple-element.40), channel_id=1, source_target_pairs={{0,1},{1,2},{2,3},{3,4},{4,5},{5,6},{6,7},{7,8},{8,9},{9,10},{10,1... | collective-permute-start | bytes 294920 | tf_op jit(solution)/shard_map/ppermute | solution.py:18
where the time goes:
time: 651 us; the launch traced here: 645 us
  other arithmetic  326 us (50%)
  local copies, waits for them, and re-layouts  131 us (20%)
  waiting for transfers between devices  103 us (16%)
  matrix products  55.7 us (9%)
  starting transfers between devices  28.2 us (4%)
    add x2, other arithmetic, body(): press = press + step  129 us
    all_to_all x1, waiting for transfers between devices, body(): lax.all_to_all(planes, 'wide', split_axis=1, concat_axis=0, tiled=True)  94.1 us
    convert_element_type x1, other arithmetic, body(): return press.astype(jnp.bfloat16)  71.4 us
    broadcast_in_dim x1, local copies, waits for them, and re-layouts, body(): planes = lax.map(both_axes, own_modes)  52.2 us
    dot_general x1, other arithmetic, rows_for(): jnp.dot(basis_x, coeff, preferred_element_type=jnp.float32)  45.8 us
    dot_general x1, matrix products, rows_for(): jnp.dot(basis_x, coeff, preferred_element_type=jnp.float32)  42.6 us
    dot_general x1, other arithmetic, contract_last(): lax.dot_general(left, table, (((left.ndim - 1,), (1,)), ((), ())), prefer...  36.9 us
    unnamed x1, other arithmetic  31.9 us
  transfers between devices with their start and end apart: 9, of which 4 were waited for; matrix products, arithmetic and copies ran while one was open for 3% of the time, Pallas kernels for 0%

commit v1 on v0

--- a/solution.py
+++ b/solution.py
@@ -1,8 +1,11 @@
+import functools
 import math
 
 import jax
 import jax.numpy as jnp
 from jax import lax
+from jax.experimental import pallas as pl
+from jax.experimental.pallas import tpu as pltpu
 from jax.sharding import PartitionSpec as P
 
 LEN_X = 1536
@@ -81,7 +84,7 @@
     return total
 
 
-def body(stream_index, forcing):
+def plain_body(stream_index, forcing):
     depth = forcing.shape[0]
     planes_here = depth // lax.axis_size("wide")
     stream_key = scramble(stream_index[0] ^ 1540483477)
@@ -124,9 +127,472 @@
     return press.astype(jnp.bfloat16)
 
 
+WIDE = 16
+DEPTH = 16
+HALO = ITERS - 1
+TILE = 16
+VMEM_LIMIT = 58 << 20
+THETA = 27.9
+DELTA = 26.1
+SIN_PI = (
+    3.141592640144167, -5.16771008404795, 2.550077528430638, -0.5982912997813382, 0.077657661199004
+)
+MULT = 73244475
+
+
+def cos_turns(turns, amplitude, negative=False):
+    coeffs = [c * math.sqrt(2.0 * amplitude) for c in SIN_PI]
+    square = turns * turns
+    poly = coeffs[4] * square + coeffs[3]
+    for c in coeffs[2::-1]:
+        poly = poly * square + c
+    sine = poly * turns
+    return sine * sine - amplitude if negative else amplitude - sine * sine
+
+
+def turns_of(phase, period):
+    return (phase - jnp.floor(phase * (1.0 / period) + 0.5) * period) * (1.0 / period)
+
+
+def srl(value, count):
+    return lax.shift_right_logical(value, jnp.int32(count))
+
+
+def basis_into(out_ref, cos_ref, sin_ref, big_cos_ref, big_sin_ref, length, rows):
+    period = 4.0 * length
+    tiles = length // rows
+
+    def phases(table_rows, of_row, cos_out, sin_out, weighted):
+        def part(i, carry):
+            r = lax.broadcasted_iota(jnp.int32, (8, 128), 0) + i * 8
+            factor = of_row(r).astype(jnp.float32)
+            at = pl.ds(pl.multiple_of(i * 8, 8), 8)
+            for j in range(length // 128):
+                k = lax.broadcasted_iota(jnp.int32, (8, 128), 1).astype(jnp.float32) + 128.0 * j
+                phase = factor * k
+                cosine = cos_turns(turns_of(phase, period), 1.0)
+                sine = cos_turns(turns_of(phase - length, period), 1.0)
+                if weighted:
+                    weight = jnp.where(k == 0.0, math.sqrt(1.0 / length), math.sqrt(2.0 / length))
+                    cosine = cosine * weight
+                    sine = sine * weight
+                cos_out[at, j * 128 : (j + 1) * 128] = cosine
+                sin_out[at, j * 128 : (j + 1) * 128] = sine
+            return carry
+
+        lax.fori_loop(0, table_rows // 8, part, 0)
+
+    phases(rows, lambda r: 2 * r + 1, cos_ref, sin_ref, True)
+    phases(tiles, lambda t: 2 * rows * t, big_cos_ref, big_sin_ref, False)
+
+    def tile(group, carry):
+        group_at = pl.ds(pl.multiple_of(group * 8, 8), 8)
+        for j in range(length // 128):
+            cols = slice(j * 128, (j + 1) * 128)
+            big_cos = big_cos_ref[group_at, cols]
+            big_sin = big_sin_ref[group_at, cols]
+            for t in range(8):
+                at = pl.ds(pl.multiple_of((group * 8 + t) * rows, rows), rows)
+                value = cos_ref[:, cols] * big_cos[t : t + 1] - sin_ref[:, cols] * big_sin[t : t + 1]
+                out_ref[at, cols] = value.astype(jnp.bfloat16)
+        return carry
+
+    lax.fori_loop(0, tiles // 8, tile, 0)
+
+
+def coefficients_into(out_ref, key, mode_z, depth, rows):
+    const = 2.0 * math.log(2.0)
+    key_low = key & 1023
+    key_high = key & ~1023
+
+    def part(i, carry):
+        r = lax.broadcasted_iota(jnp.int32, (rows, 128), 0) + i * rows
+        at = pl.ds(pl.multiple_of(i * rows, rows), rows)
+        freq_x = r.astype(jnp.float32) * (math.pi / LEN_X)
+        freq_z = mode_z.astype(jnp.float32) * (math.pi / depth)
+        row_part = (0.05 + freq_x * freq_x + freq_z * freq_z) * -const
+        base = (r + mode_z * LEN_X) * (2 * LEN_Y)
+        lane = lax.broadcasted_iota(jnp.int32, (1, 128), 1)
+        for j in range(LEN_Y // 128):
+            if j % 4 == 0:
+                top = (base + j * 256) ^ key_high
+                top = top ^ srl(top, 16)
+                delta = jnp.where(((top ^ key_low) & 1) == 0, MULT, -MULT)
+            freq_y = (lane + j * 128).astype(jnp.float32) * (math.pi / LEN_Y)
+            denom = row_part + freq_y * freq_y * -const
+            a = (top ^ (((lane + (j % 4) * 128) * 2) ^ key_low)) * MULT
+            b = a + delta
+            a = (a ^ srl(a, 16)) * MULT
+            b = (b ^ srl(b, 16)) * MULT
+            a = srl(a ^ srl(a, 16), 8)
+            b = (b ^ srl(b, 16)) >> 8
+            u = a.astype(jnp.float32) * 2.0 ** (-24) + 2.0 ** (-25)
+            turns = b.astype(jnp.float32) * 2.0 ** (-24) + 2.0 ** (-25)
+            bits = jnp.minimum(jnp.log2(u), -1e-30)
+            size = bits * lax.rsqrt(bits * denom)
+            value = size * cos_turns(turns, const, negative=True)
+            out_ref[at, j * 128 : (j + 1) * 128] = value.astype(jnp.bfloat16)
+        return carry
+
+    lax.fori_loop(0, LEN_X // rows, part, 0)
+
+
+def transform_into(out_ref, left_ref, coef_ref, rows_ref, basis_ref):
+    for n in range(0, LEN_Y, 256):
+        cols = slice(n, n + 256)
+        rows_ref[:, cols] = jnp.dot(
+            left_ref[...], coef_ref[:, cols], preferred_element_type=jnp.float32
+        ).astype(jnp.bfloat16)
+    for n in range(0, LEN_Y, 256):
+        cols = slice(n, n + 256)
+        out_ref[:, cols] = contract_last(rows_ref[...], basis_ref[cols, :]).astype(jnp.bfloat16)
+
+
+def first_planes_kernel(
+    scalars, out_ref, basis_out, basis, coef, rows, cos_a, sin_a, cos_b, sin_b, sem, *, depth, count
+):
+    basis_into(basis, cos_a, sin_a, cos_b, sin_b, LEN_X, 64)
+    copy = pltpu.make_async_copy(basis, basis_out, sem)
+    copy.start()
+    coefficients_into(coef, scalars[0], scalars[1], depth, 64)
+    left = basis.at[pl.ds(pl.multiple_of(scalars[2], count), count), :]
+    transform_into(out_ref, left, coef, rows, basis)
+    copy.wait()
+
+
+def first_planes(scalars, depth, count):
+    return pl.pallas_call(
+        functools.partial(first_planes_kernel, depth=depth, count=count),
+        in_specs=[pl.BlockSpec(memory_space=pltpu.SMEM)],
+        out_specs=[pl.BlockSpec(memory_space=pltpu.VMEM), pl.BlockSpec(memory_space=pl.ANY)],
+        out_shape=[
+            jax.ShapeDtypeStruct((count, LEN_Y), jnp.bfloat16),
+            jax.ShapeDtypeStruct((LEN_X, LEN_X), jnp.bfloat16),
+        ],
+        scratch_shapes=[
+            pltpu.VMEM((LEN_X, LEN_X), jnp.bfloat16),
+            pltpu.VMEM((LEN_X, LEN_Y), jnp.bfloat16),
+            pltpu.VMEM((count, LEN_Y), jnp.bfloat16),
+            pltpu.VMEM((64, LEN_X), jnp.float32),
+            pltpu.VMEM((64, LEN_X), jnp.float32),
+            pltpu.VMEM((LEN_X // 64, LEN_X), jnp.float32),
+            pltpu.VMEM((LEN_X // 64, LEN_X), jnp.float32),
+            pltpu.SemaphoreType.DMA,
+        ],
+        compiler_params=pltpu.CompilerParams(vmem_limit_bytes=VMEM_LIMIT),
+        name="first_planes",
+    )(scalars)
+
+
+def more_planes_kernel(scalars, basis_in, out_ref, basis, left, coef, rows, sem, *, depth, count):
+    half = count // 2
+    copies = [pltpu.make_async_copy(basis_in, basis, sem.at[0])]
+    for n in range(2):
+        source = basis_in.at[pl.ds(pl.multiple_of(scalars[2 + n], half), half), :]
+        copies.append(pltpu.make_async_copy(source, left.at[pl.ds(n * half, half), :], sem.at[1 + n]))
+    for copy in copies:
+        copy.start()
+    coefficients_into(coef, scalars[0], scalars[1], depth, 64)
+    for copy in copies:
+        copy.wait()
+    transform_into(out_ref, left, coef, rows, basis)
+
+
+def more_planes(scalars, basis, depth, count):
+    return pl.pallas_call(
+        functools.partial(more_planes_kernel, depth=depth, count=count),
+        in_specs=[pl.BlockSpec(memory_space=pltpu.SMEM), pl.BlockSpec(memory_space=pl.ANY)],
+        out_specs=pl.BlockSpec(memory_space=pltpu.VMEM),
+        out_shape=jax.ShapeDtypeStruct((count, LEN_Y), jnp.bfloat16),
+        scratch_shapes=[
+            pltpu.VMEM((LEN_X, LEN_X), jnp.bfloat16),
+            pltpu.VMEM((count, LEN_X), jnp.bfloat16),
+            pltpu.VMEM((LEN_X, LEN_Y), jnp.bfloat16),
+            pltpu.VMEM((count, LEN_Y), jnp.bfloat16),
+            pltpu.SemaphoreType.DMA((3,)),
+        ],
+        compiler_params=pltpu.CompilerParams(vmem_limit_bytes=VMEM_LIMIT),
+        name="more_planes",
+    )(scalars, basis)
+
+
+def swap_matrix(depth):
+    size = depth * TILE
+    row = lax.broadcasted_iota(jnp.int32, (size, size), 0)
+    col = lax.broadcasted_iota(jnp.int32, (size, size), 1)
+    return (col == (row % depth) * TILE + row // depth).astype(jnp.bfloat16)
+
+
+def turn_kernel(matrix, in_ref, out_ref):
+    tile = in_ref[...].reshape(matrix.shape[1], LEN_Y)
+    turned = jnp.dot(matrix[...], tile, preferred_element_type=jnp.float32)
+    out_ref[...] = turned.astype(jnp.bfloat16).reshape(out_ref.shape)
+
+
+def turn(matrix, forcing):
+    depth, count, _ = forcing.shape
+    return pl.pallas_call(
+        turn_kernel,
+        grid=(count // TILE,),
+        in_specs=[
+            pl.BlockSpec(matrix.shape, lambda i: (0, 0)),
+            pl.BlockSpec((depth, TILE, LEN_Y), lambda i: (0, i, 0)),
+        ],
+        out_specs=pl.BlockSpec((TILE, depth, LEN_Y), lambda i: (i, 0, 0)),
+        out_shape=jax.ShapeDtypeStruct((count, depth, LEN_Y), jnp.bfloat16),
+        compiler_params=pltpu.CompilerParams(vmem_limit_bytes=VMEM_LIMIT),
+        name="turn",
+    )(matrix, forcing)
+
+
+def perm_kernel(matrix, a_ref, b_ref, c_ref, out_ref):
+    field = None
+    start = 0
+    for ref in (a_ref, b_ref, c_ref):
+        size = ref.shape[0] * TILE
+        part = jnp.dot(
+            matrix[:, start : start + size],
+            ref[...].reshape(size, LEN_Y),
+            preferred_element_type=jnp.float32,
+        )
+        field = part if field is None else field + part
+        start += size
+    out_ref[...] = jnp.exp(1.5 * jnp.tanh(2.0 * field)).astype(jnp.bfloat16).reshape(out_ref.shape)
+
+
+def permeability(matrix, parts):
+    count = parts[0].shape[1]
+    depth = sum(part.shape[0] for part in parts)
+    return pl.pallas_call(
+        perm_kernel,
+        grid=(count // TILE,),
+        in_specs=[pl.BlockSpec(matrix.shape, lambda i: (0, 0))]
+        + [pl.BlockSpec((part.shape[0], TILE, LEN_Y), lambda i: (0, i, 0)) for part in parts],
+        out_specs=pl.BlockSpec((TILE, depth, LEN_Y), lambda i: (i, 0, 0)),
+        out_shape=jax.ShapeDtypeStruct((count, depth, LEN_Y), jnp.bfloat16),
+        compiler_params=pltpu.CompilerParams(vmem_limit_bytes=VMEM_LIMIT),
+        name="permeability",
+    )(matrix, *parts)
+
+
+def chebyshev():
+    sigma = THETA / DELTA
+    rho = 1.0 / sigma
+    pairs = []
+    for _ in range(ITERS - 1):
+        rho_next = 1.0 / (2.0 * sigma - rho)
+        pairs.append((rho_next * rho, 2.0 * rho_next / DELTA))
+        rho = rho_next
+    return pairs
+
+
+def solve_kernel(
+    flags, swap, f_in, f_low, f_high, k_in, k_low, k_high, out_ref, f, kb, kh, pa, pb, tile, flux, sem
+):
+    count, depth, _ = f_in.shape
+    total = count + 2 * HALO
+    copies = []
+    for n, (low, mid, high, target) in enumerate(((f_low, f_in, f_high, f), (k_low, k_in, k_high, kb))):
+        for m, (ref, start) in enumerate(((low, 0), (mid, HALO), (high, HALO + count))):
+            copies.append(
+                pltpu.make_async_copy(ref, target.at[pl.ds(start, ref.shape[0])], sem.at[3 * n + m])
+            )
+    for copy in copies:
+        copy.start()
+    for copy in copies:
+        copy.wait()
+
+    def prepare(e, carry):
+        kh[e] = 0.5 * kb[e].astype(jnp.float32)
+        pa[e] = f[e].astype(jnp.float32) * (1.0 / THETA)
+        return carry
+
+    lax.fori_loop(0, total, prepare, 0)
+    lane = lax.broadcasted_iota(jnp.int32, (depth, 128), 1)
+    level = lax.broadcasted_iota(jnp.int32, (depth, 128), 0)
+    blocks = LEN_Y // 128
+
+    def cols(j):
+        return slice(j * 128, (j + 1) * 128)
+
+    def up(value):
+        return jnp.where(level == depth - 1, 0.0, pltpu.roll(value, depth - 1, 0))
+
+    def iteration(first, last, src, store):
+        for j in range(blocks):
+            k_here = kh[first - 1, :, cols(j)]
+            k_next = kh[first, :, cols(j)]
+            flux[:, cols(j)] = (k_here + k_next) * (src[first - 1, :, cols(j)] - src[first, :, cols(j)])
+
+        def row(e, carry):
+            p = src[e, :, cols(0)]
+            k = kh[e, :, cols(0)]
+            p_turn = pltpu.roll(p, 127, 1)
+            k_turn = pltpu.roll(k, 127, 1)
+            before = None
+            for j in range(blocks):
+                if j + 1 < blocks:
+                    p_after = src[e, :, cols(j + 1)]
+                    k_after = kh[e, :, cols(j + 1)]
+                    p_after_turn = pltpu.roll(p_after, 127, 1)
+                    k_after_turn = pltpu.roll(k_after, 127, 1)
+                else:
+                    p_after = k_after = None
+                    p_after_turn = k_after_turn = 0.0
+                p_right = jnp.where(lane == 127, p_after_turn, p_turn)
+                k_right = jnp.where(lane == 127, k_after_turn, k_turn)
+                flow_y = (k + k_right) * (p - p_right)
+                flow_turn = pltpu.roll(flow_y, 1, 1)
+                left = jnp.where(lane == 0, -k * p if before is None else before, flow_turn)
+                before = flow_turn
+                flow_z = (k + up(k)) * (p - up(p))
+                under = jnp.where(level == 0, -k * p, pltpu.roll(flow_z, 1, 0))
+                flow_x = (k + kh[e + 1, :, cols(j)]) * (p - src[e + 1, :, cols(j)])
+                out = (flow_x - flux[:, cols(j)]) + (flow_y - left) + (flow_z - under)
+                flux[:, cols(j)] = flow_x
+                store(e, j, p, out)
+                p, k, p_turn, k_turn = p_after, k_after, p_after_turn, k_after_turn
+            return carry
+
+        return row
+
+    def clear(ref, first, last):
+        @pl.when(flags[0] == 0)
+        def _():
+            for e in range(first, HALO):
+                ref[e] = jnp.zeros(ref.shape[1:], ref.dtype)
+
+        @pl.when(flags[1] == 0)
+        def _():
+            for e in range(HALO + count, last):
+                ref[e] = jnp.zeros(ref.shape[1:], ref.dtype)
+
+    (a1, b1), (a2, b2), (a3, b3) = chebyshev()
+
+    def store_one(e, j, p, out):
+        pb[e, :, cols(j)] = (1.0 + a1 + b1 * THETA) * p - b1 * out
+
+    def store_two(e, j, p, out):
+        old = f[e, :, cols(j)].astype(jnp.float32)
+        pa[e, :, cols(j)] = (1.0 + a2) * p + (b2 - a2 / THETA) * old - b2 * out
+
+    lax.fori_loop(1, total - 1, iteration(1, total - 1, pa, store_one), 0)
+    clear(pb, 1, total - 1)
+    lax.fori_loop(2, total - 2, iteration(2, total - 2, pb, store_two), 0)
+    clear(pa, 2, total - 2)
+
+    def store_three(e, j, p, out):
+        source = f[e, :, cols(j)].astype(jnp.float32)
+        value = (1.0 + a3) * p - a3 * pb[e, :, cols(j)] + b3 * (source - out)
+        tile[(e - HALO) % TILE, :, cols(j)] = value.astype(jnp.bfloat16)
+
+    row = iteration(HALO, total - HALO, pa, store_three)
+
+    def strip(t, carry):
+        lax.fori_loop(HALO + t * TILE, HALO + (t + 1) * TILE, row, 0)
+        turned = jnp.dot(
+            swap[...], tile[...].reshape(TILE * depth, LEN_Y), preferred_element_type=jnp.float32
+        )
+        out_ref[:, pl.ds(pl.multiple_of(t * TILE, TILE), TILE), :] = turned.astype(jnp.bfloat16).reshape(
+            depth, TILE, LEN_Y
+        )
+        return carry
+
+    lax.fori_loop(0, count // TILE, strip, 0)
+
+
+def solve(flags, swap, f_parts, k_parts):
+    count, depth, _ = f_parts[0].shape
+    total = count + 2 * HALO
+    anywhere = pl.BlockSpec(memory_space=pl.ANY)
+    return pl.pallas_call(
+        solve_kernel,
+        in_specs=[pl.BlockSpec(memory_space=pltpu.SMEM), pl.BlockSpec(memory_space=pltpu.VMEM)]
+        + [anywhere] * 6,
+        out_specs=pl.BlockSpec(memory_space=pltpu.VMEM),
+        out_shape=jax.ShapeDtypeStruct((depth, count, LEN_Y), jnp.bfloat16),
+        scratch_shapes=[
+            pltpu.VMEM((total, depth, LEN_Y), jnp.bfloat16),
+            pltpu.VMEM((total, depth, LEN_Y), jnp.bfloat16),
+            pltpu.VMEM((total, depth, LEN_Y), jnp.float32),
+            pltpu.VMEM((total, depth, LEN_Y), jnp.float32),
+            pltpu.VMEM((total, depth, LEN_Y), jnp.float32),
+            pltpu.VMEM((TILE, depth, LEN_Y), jnp.bfloat16),
+            pltpu.VMEM((depth, LEN_Y), jnp.float32),
+            pltpu.SemaphoreType.DMA((6,)),
+        ],
+        compiler_params=pltpu.CompilerParams(vmem_limit_bytes=VMEM_LIMIT),
+        name="solve",
+    )(flags, swap, *f_parts, *k_parts)
+
+
+def edges(block):
+    forward = [(i, i + 1) for i in range(WIDE - 1)]
+    backward = [(target, source) for source, target in forward]
+    low = lax.ppermute(block[-HALO:], "wide", forward)
+    high = lax.ppermute(block[:HALO], "wide", backward)
+    return block, low, high
+
+
+def basis_columns(modes, length):
+    row_idx = lax.broadcasted_iota(jnp.int32, (length, length), 0)
+    phase = (2 * row_idx + 1) * modes[None, :] % (4 * length)
+    angle = phase.astype(jnp.float32) * (math.pi / (2.0 * length))
+    weights = jnp.where(modes[None, :] == 0, math.sqrt(1.0 / length), math.sqrt(2.0 / length))
+    return (weights * jnp.cos(angle)).astype(jnp.bfloat16)
+
+
+def body(stream_index, forcing):
+    depth, count, _ = forcing.shape
+    index = lax.axis_index("wide")
+    core = index % 2
+    side = index // 2 % 2
+    far = index // 4 % 2
+    color = side ^ far
+    key = scramble(stream_index[0] ^ 1540483477)
+    own = index // 2 * 2 * count
+    shared = DEPTH // 2 + 4 * color + 2 * core
+
+    first, basis = first_planes(
+        jnp.stack([key, index % 8, index // 8 * 8 * count]).astype(jnp.int32), depth, 8 * count
+    )
+    groups = [list(range(8)), list(range(8, 16))]
+    part_a = lax.all_to_all(
+        first.reshape(8, count, LEN_Y), "wide", 0, 0, axis_index_groups=groups, tiled=True
+    )
+
+    def pairwise(mode, other, basis, groups):
+        low = jnp.minimum(own, other)
+        high = jnp.maximum(own, other)
+        out = more_planes(jnp.stack([key, mode, low, high]).astype(jnp.int32), basis, depth, 4 * count)
+        part = lax.all_to_all(
+            out.reshape(4, count, LEN_Y), "wide", 0, 0, axis_index_groups=groups, tiled=True
+        )
+        return part
+
+    far_groups = [[s, s + 1, s + 4, s + 5] for s in (0, 2, 8, 10)]
+    side_groups = [[s, s + 1, s + 2, s + 3] for s in (0, 4, 8, 12)]
+    part_b = pairwise(shared, (index ^ 4) // 2 * 2 * count, basis, far_groups)
+    part_c = pairwise(shared + 1, (index ^ 2) // 2 * 2 * count, basis, side_groups)
+    slot = jnp.arange(4, dtype=jnp.int32)
+    modes_b = DEPTH // 2 + 4 * (slot // 2 ^ side) + 2 * (slot % 2)
+    modes_c = DEPTH // 2 + 4 * (slot // 2 ^ far) + 2 * (slot % 2) + 1
+    modes = jnp.concatenate([jnp.arange(8, dtype=jnp.int32), modes_b, modes_c])
+
+    swap = swap_matrix(depth)
+    f_parts = edges(turn(swap, forcing))
+    basis_z = basis_columns(modes, depth)
+    eye = jnp.eye(TILE, dtype=jnp.bfloat16)
+    mixing = (eye[:, None, None, :] * basis_z[None, :, :, None]).reshape(TILE * depth, depth * TILE)
+    k_parts = edges(permeability(mixing, [part_a, part_b, part_c]))
+    flags = jnp.stack([index > 0, index < WIDE - 1]).astype(jnp.int32)
+    return solve(flags, swap, f_parts, k_parts)
+
+
 def solution(mesh):
+    special = mesh.shape["wide"] == WIDE
     return jax.shard_map(
-        body,
+        body if special else plain_body,
         mesh=mesh,
         in_specs=(P("group"), P("group", "wide", None)),
         out_specs=P("group", "wide", None),

time: 651 us -> 220 us (0.34)
  other arithmetic: 326 us -> 3.22 us
  Pallas kernels: 0 us -> 154 us
  local copies, waits for them, and re-layouts: 131 us -> 6.46 us
  waiting for transfers between devices: 103 us -> 17.2 us
  matrix products: 55.7 us -> 0 us
  blocking collectives: 0 us -> 20.2 us
  starting transfers between devices: 28.2 us -> 16.8 us
    pallas_call x0 -> x6, Pallas kernels: none -> 154 us  [the longest x1 70.4 us: solve(): pl.pallas_call(solve_kernel, in_specs=[pl.BlockSpec(memory_space=pltpu.SM...]
    add x4 -> x3, other arithmetic: 129 us -> 0.02 us  [the longest x1 0.01 us: body(): modes_c = DEPTH // 2 + 4 * (slot // 2 ^ far) + 2 * (slot % 2) + 1]
    dot_general x2 -> x0, other arithmetic: 82.7 us -> none  [the longest x1 45.8 us: rows_for(): jnp.dot(basis_x, coeff, preferred_element_type=jnp.float32)]
    all_to_all x1 -> x2, waiting for transfers between devices: 94.1 us -> 12.9 us  [the longest x1 12.9 us: body(): lax.all_to_all(first.reshape(8, count, LEN_Y), 'wide', 0, 0, axis_index_g...]
    convert_element_type x2 -> x4, other arithmetic: 72.1 us -> 1.69 us  [the longest x1 0.94 us: swap_matrix(): return (col == row % depth * TILE + row // depth).astype(jnp.bfloat16)]
    dot_general x3 -> x0, matrix products: 55.7 us -> none  [the longest x1 42.6 us: rows_for(): jnp.dot(basis_x, coeff, preferred_element_type=jnp.float32)]
    broadcast_in_dim x1 -> x0, local copies, waits for them, and re-layouts: 52.2 us -> none  [body(): planes = lax.map(both_axes, own_modes)]
    unnamed x1 -> x0, other arithmetic: 31.9 us -> none
  transfers between devices with their start and end apart: 9 -> 6, of which waited for: 4 -> 2; matrix products, arithmetic and copies ran while one was open for 3% -> 3% of each run, Pallas kernels for 0% -> 16%
where the time goes in v1:
time: 220 us; the launch traced here: 219 us
  Pallas kernels  154 us (70%)
  blocking collectives  20.2 us (9%)
  waiting for transfers between devices  17.2 us (8%)
  starting transfers between devices  16.8 us (8%)
  local copies, waits for them, and re-layouts  6.46 us (3%)
  other arithmetic  3.22 us (1%)
    pallas_call x1, Pallas kernels, solve(): pl.pallas_call(solve_kernel, in_specs=[pl.BlockSpec(memory_space=pltpu.SM...  70.4 us
    pallas_call x2, Pallas kernels, more_planes(): pl.pallas_call(functools.partial(more_planes_kernel, depth=depth, count=c...  39.9 us
    pallas_call x1, Pallas kernels, first_planes(): pl.pallas_call(functools.partial(first_planes_kernel, depth=depth, count=...  27.7 us
    all_to_all x1, blocking collectives, pairwise(): lax.all_to_all(out.reshape(4, count, LEN_Y), 'wide', 0, 0, axis_index_gro...  20.2 us
    all_to_all x1, waiting for transfers between devices, body(): lax.all_to_all(first.reshape(8, count, LEN_Y), 'wide', 0, 0, axis_index_g...  12.9 us
    pallas_call x1, Pallas kernels, permeability(): pl.pallas_call(perm_kernel, grid=(count // TILE,), in_specs=[pl.BlockSpec...  8.94 us
    pallas_call x1, Pallas kernels, turn(): pl.pallas_call(turn_kernel, grid=(count // TILE,), in_specs=[pl.BlockSpec...  6.97 us
    ppermute x2, starting transfers between devices, edges(): high = lax.ppermute(block[:HALO], 'wide', backward)  5.1 us
  transfers between devices with their start and end apart: 6, of which 2 were waited for; matrix products, arithmetic and copies ran while one was open for 3% of the time, Pallas kernels for 16%

profile of v1, /device:TPU:18, one launch (start us, length us, event | category | flops | bytes accessed | tf_op | source)
XLA Modules:
  0.0 218.8 jit_solution(3647191388617785963)
XLA Ops:
  0.7 0.7 pad_add_fusion.1.scalars
  1.3 27.7 %first_planes.1 = (bf16[768,1536]{1,0:T(8,128)(2,1)}, bf16[1536,1536]{1,0:T(8,128)(2,1)}) custom-call(s32[3]{0:T(128)} %pad_add_fusion.1.scalars), custom_call_target="tpu_custom_call" | custom-call | tf_op jit(solution)/shard_map/first_planes/pallas_call | solution.py:264
  29.1 0.6 pad_add_fusion.2
  29.7 19.9 %more_planes.3 = bf16[384,1536]{1,0:T(8,128)(2,1)} custom-call(s32[4]{0:T(128)} %get-tuple-element.24.scalars, bf16[1536,1536]{1,0:T(8,128)(2,1)} %get-tuple-element.8.basis_in), custom_call_target="tpu_custom_call" | custom-call | tf_op jit(solution)/shard_map/more_planes/pallas_call | solution.py:302
  49.6 3.5 %all-to-all-start.2 = ((bf16[4,96,1536]{2,1,0:T(8,128)(2,1)}), bf16[4,96,1536]{2,1,0:T(8,128)(2,1)S(1)}, u32[]{:S(2)}, u32[]{:S(2)}) async-start(bf16[4,96,1536]{2,1,0:T(8,128)(2,1)} %bitcast.17), calls=%async_computation.2 | async-start | bytes 2359296 | tf_op jit(solution)/shard_map/all_to_all | solution.py:568
  53.2 20.0 %more_planes.2 = bf16[384,1536]{1,0:T(8,128)(2,1)} custom-call(s32[4]{0:T(128)} %get-tuple-element.23.scalars, bf16[1536,1536]{1,0:T(8,128)(2,1)} %get-tuple-element.8.basis_in), custom_call_target="tpu_custom_call" | custom-call | tf_op jit(solution)/shard_map/more_planes/pallas_call | solution.py:302
  73.1 20.2 %all_to_all.15.b_ref = bf16[4,96,1536]{2,1,0:T(8,128)(2,1)} all-to-all(bf16[4,96,1536]{2,1,0:T(8,128)(2,1)} %bitcast.18), channel_id=1, replica_groups={{0,1,4,5},{2,3,6,7},{8,9,12,13},{10,11,14,15},{16,17,20,21},{18,19,22,2..., dimensions={0} | all-to-all | bytes 2359296 | tf_op jit(solution)/shard_map/all_to_all | solution.py:568
  93.3 3.8 %all-to-all-start = ((bf16[8,96,1536]{2,1,0:T(8,128)(2,1)}), bf16[8,96,1536]{2,1,0:T(8,128)(2,1)S(1)}, u32[]{:S(2)}, u32[]{:S(2)}) async-start(bf16[8,96,1536]{2,1,0:T(8,128)(2,1)} %bitcast.19), calls=%async_computation | async-start | bytes 4718592 | tf_op jit(solution)/shard_map/all_to_all | solution.py:560
  97.2 0.9 fusion.matrix.swap
  98.1 7.0 %turn.1.f_in = bf16[96,16,1536]{2,1,0:T(8,128)(2,1)} custom-call(bf16[256,256]{1,0:T(8,128)(2,1)} %fusion.matrix.swap, bf16[16,96,1536]{2,1,0:T(8,128)(2,1)} %in_ref.1), custom_call_target="tpu_custom_call" | custom-call | tf_op jit(solution)/shard_map/turn/pallas_call | solution.py:334
  105.1 1.7 fusion.12
  106.8 3.2 %collective-permute-start.1 = (bf16[3,16,1536]{2,1,0:T(8,128)(2,1)}, bf16[3,16,1536]{2,1,0:T(8,128)(2,1)S(1)}, u32[]{:S(2)}, u32[]{:S(2)}) collective-permute-start(bf16[3,16,1536]{2,1,0:T(8,128)(2,1)} %get-tuple-element.13), channel_id=1, source_target_pairs={{1,0},{2,1},{3,2},{4,3},{5,4},{6,5},{7,6},{8,7},{9,8},{10,9},{11,1... | collective-permute-start | bytes 442376 | tf_op jit(solution)/shard_map/ppermute | solution.py:533
  110.0 1.9 collective-permute-start
  112.4 1.6 mul.130.matrix
  114.0 12.9 %all-to-all-done.a_ref = bf16[8,96,1536]{2,1,0:T(8,128)(2,1)S(1)} async-done(((bf16[8,96,1536]{2,1,0:T(8,128)(2,1)}), bf16[8,96,1536]{2,1,0:T(8,128)(2,1)S(1)}, u32[]{:S(2)}, u32[]{:S(2)}) %all-to-all-start) | async-done | bytes 2359328 | tf_op jit(solution)/shard_map/all_to_all | solution.py:560
  127.0 1.4 copy-done
  128.4 8.9 %permeability.1.k_in = bf16[96,16,1536]{2,1,0:T(8,128)(2,1)} custom-call(bf16[256,256]{1,0:T(8,128)(2,1)} %mul.130.matrix, bf16[8,96,1536]{2,1,0:T(8,128)(2,1)} %copy-done, bf16[4,96,1536]{2,1,0:T(8,128)(2,1)} %all_to_all.15.b_ref, bf16[4,96,1536]{2,1,0:T(8,128)(2,1)} %copy-done.1), custom_call_target="tpu_custom_call" | custom-call | tf_op jit(solution)/shard_map/permeability/pallas_call | solution.py:366
  137.3 1.0 fusion.11
  138.3 1.9 collective-permute-start.3
  140.2 2.4 %collective-permute-start.2 = (bf16[3,16,1536]{2,1,0:T(8,128)(2,1)S(1)}, bf16[3,16,1536]{2,1,0:T(8,128)(2,1)S(1)}, u32[]{:S(2)}, u32[]{:S(2)}) collective-permute-start(bf16[3,16,1536]{2,1,0:T(8,128)(2,1)S(1)} %get-tuple-element.12), channel_id=1, source_target_pairs={{0,1},{1,2},{2,3},{3,4},{4,5},{5,6},{6,7},{7,8},{8,9},{9,10},{10,1... | collective-permute-start | bytes 442376 | tf_op jit(solution)/shard_map/ppermute | solution.py:532
  142.7 0.6 add_convert_fusion.flags
  143.3 4.3 %collective-permute-done.2.k_low = bf16[3,16,1536]{2,1,0:T(8,128)(2,1)S(1)} collective-permute-done((bf16[3,16,1536]{2,1,0:T(8,128)(2,1)S(1)}, bf16[3,16,1536]{2,1,0:T(8,128)(2,1)S(1)}, u32[]{:S(2)}, u32[]{:S(2)}) %collective-permute-start.2) | collective-permute-done | bytes 147488 | tf_op jit(solution)/shard_map/ppermute | solution.py:532
  147.6 0.7 copy-done.4
  148.3 70.4 %solve.1 = bf16[16,96,1536]{2,1,0:T(8,128)(2,1)} custom-call(s32[2]{0:T(128)} %add_convert_fusion.flags, bf16[256,256]{1,0:T(8,128)(2,1)} %fusion.matrix.swap, bf16[96,16,1536]{2,1,0:T(8,128)(2,1)} %turn.1.f_in, bf16[3,16,1536]{2,1,0:T(8,128)(2,1)} %collective-permute-done.f_low, bf16[3,16,1536]{2,1,0:T(8,128)(2,1)} %copy-done.2, ...), custom_call_target="tpu_custom_call" | custom-call | tf_op jit(solution)/shard_map/solve/pallas_call | solution.py:508
  (22 shorter events, 0.4 us)
Async XLA Ops:
  49.6 23.5 %all-to-all-start.2 = ((bf16[4,96,1536]{2,1,0:T(8,128)(2,1)}), bf16[4,96,1536]{2,1,0:T(8,128)(2,1)S(1)}, u32[]{:S(2)}, u32[]{:S(2)}) async-start(bf16[4,96,1536]{2,1,0:T(8,128)(2,1)} %bitcast.17), calls=%async_computation.2 | async-start | bytes 2359296 | tf_op jit(solution)/shard_map/all_to_all | solution.py:568
  73.1 32.0 %copy-start.1 = (bf16[4,96,1536]{2,1,0:T(8,128)(2,1)}, bf16[4,96,1536]{2,1,0:T(8,128)(2,1)S(1)}, u32[]{:S(2)}) copy-start(bf16[4,96,1536]{2,1,0:T(8,128)(2,1)S(1)} %all-to-all-done.2.c_ref) | copy-start | bytes 3538948
  93.3 33.6 %all-to-all-start = ((bf16[8,96,1536]{2,1,0:T(8,128)(2,1)}), bf16[8,96,1536]{2,1,0:T(8,128)(2,1)S(1)}, u32[]{:S(2)}, u32[]{:S(2)}) async-start(bf16[8,96,1536]{2,1,0:T(8,128)(2,1)} %bitcast.19), calls=%async_computation | async-start | bytes 4718592 | tf_op jit(solution)/shard_map/all_to_all | solution.py:560
  106.8 36.4 %collective-permute-start.1 = (bf16[3,16,1536]{2,1,0:T(8,128)(2,1)}, bf16[3,16,1536]{2,1,0:T(8,128)(2,1)S(1)}, u32[]{:S(2)}, u32[]{:S(2)}) collective-permute-start(bf16[3,16,1536]{2,1,0:T(8,128)(2,1)} %get-tuple-element.13), channel_id=1, source_target_pairs={{1,0},{2,1},{3,2},{4,3},{5,4},{6,5},{7,6},{8,7},{9,8},{10,9},{11,1... | collective-permute-start | bytes 442376 | tf_op jit(solution)/shard_map/ppermute | solution.py:533
  110.0 33.2 %collective-permute-start = (bf16[3,16,1536]{2,1,0:T(8,128)(2,1)}, bf16[3,16,1536]{2,1,0:T(8,128)(2,1)}, u32[]{:S(2)}, u32[]{:S(2)}) collective-permute-start(bf16[3,16,1536]{2,1,0:T(8,128)(2,1)} %get-tuple-element.14), channel_id=1, source_target_pairs={{0,1},{1,2},{2,3},{3,4},{4,5},{5,6},{6,7},{7,8},{8,9},{9,10},{10,1... | collective-permute-start | bytes 442376 | tf_op jit(solution)/shard_map/ppermute | solution.py:532
  127.0 1.4 copy-start
  138.3 5.0 %collective-permute-start.3 = (bf16[3,16,1536]{2,1,0:T(8,128)(2,1)S(1)}, bf16[3,16,1536]{2,1,0:T(8,128)(2,1)S(1)}, u32[]{:S(2)}, u32[]{:S(2)}) collective-permute-start(bf16[3,16,1536]{2,1,0:T(8,128)(2,1)S(1)} %get-tuple-element.11), channel_id=1, source_target_pairs={{1,0},{2,1},{3,2},{4,3},{5,4},{6,5},{7,6},{8,7},{9,8},{10,9},{11,1... | collective-permute-start | bytes 442376 | tf_op jit(solution)/shard_map/ppermute | solution.py:533
  140.2 7.4 %collective-permute-start.2 = (bf16[3,16,1536]{2,1,0:T(8,128)(2,1)S(1)}, bf16[3,16,1536]{2,1,0:T(8,128)(2,1)S(1)}, u32[]{:S(2)}, u32[]{:S(2)}) collective-permute-start(bf16[3,16,1536]{2,1,0:T(8,128)(2,1)S(1)} %get-tuple-element.12), channel_id=1, source_target_pairs={{0,1},{1,2},{2,3},{3,4},{4,5},{5,6},{6,7},{7,8},{8,9},{9,10},{10,1... | collective-permute-start | bytes 442376 | tf_op jit(solution)/shard_map/ppermute | solution.py:532
  143.3 4.3 %copy-start.2 = (bf16[3,16,1536]{2,1,0:T(8,128)(2,1)}, bf16[3,16,1536]{2,1,0:T(8,128)(2,1)S(1)}, u32[]{:S(2)}) copy-start(bf16[3,16,1536]{2,1,0:T(8,128)(2,1)S(1)} %collective-permute-done.1.f_high) | copy-start | bytes 442372
  143.3 4.3 %copy-start.3 = (bf16[3,16,1536]{2,1,0:T(8,128)(2,1)}, bf16[3,16,1536]{2,1,0:T(8,128)(2,1)S(1)}, u32[]{:S(2)}) copy-start(bf16[3,16,1536]{2,1,0:T(8,128)(2,1)S(1)} %collective-permute-done.3.k_high) | copy-start | bytes 442372
  147.6 0.7 copy-start.4

commit v2 on v1

--- a/solution.py
+++ b/solution.py
@@ -130,6 +130,7 @@
 WIDE = 16
 DEPTH = 16
 HALO = ITERS - 1
+PARTS = 4
 TILE = 16
 VMEM_LIMIT = 58 << 20
 THETA = 27.9
@@ -237,15 +238,18 @@
     lax.fori_loop(0, LEN_X // rows, part, 0)
 
 
-def transform_into(out_ref, left_ref, coef_ref, rows_ref, basis_ref):
+def transform_into(out_refs, left_ref, coef_ref, rows_ref, basis_ref):
     for n in range(0, LEN_Y, 256):
         cols = slice(n, n + 256)
         rows_ref[:, cols] = jnp.dot(
             left_ref[...], coef_ref[:, cols], preferred_element_type=jnp.float32
         ).astype(jnp.bfloat16)
+    size = rows_ref.shape[0] // len(out_refs)
     for n in range(0, LEN_Y, 256):
         cols = slice(n, n + 256)
-        out_ref[:, cols] = contract_last(rows_ref[...], basis_ref[cols, :]).astype(jnp.bfloat16)
+        value = contract_last(rows_ref[...], basis_ref[cols, :]).astype(jnp.bfloat16)
+        for m, out_ref in enumerate(out_refs):
+            out_ref[:, cols] = value[m * size : (m + 1) * size]
 
 
 def first_planes_kernel(
@@ -256,7 +260,7 @@
     copy.start()
     coefficients_into(coef, scalars[0], scalars[1], depth, 64)
     left = basis.at[pl.ds(pl.multiple_of(scalars[2], count), count), :]
-    transform_into(out_ref, left, coef, rows, basis)
+    transform_into([out_ref], left, coef, rows, basis)
     copy.wait()
 
 
@@ -280,38 +284,42 @@
             pltpu.SemaphoreType.DMA,
         ],
         compiler_params=pltpu.CompilerParams(vmem_limit_bytes=VMEM_LIMIT),
+        cost_estimate=pl.CostEstimate(flops=25_000_000_000, transcendentals=0, bytes_accessed=8_000_000),
         name="first_planes",
     )(scalars)
 
 
-def more_planes_kernel(scalars, basis_in, out_ref, basis, left, coef, rows, sem, *, depth, count):
-    half = count // 2
-    copies = [pltpu.make_async_copy(basis_in, basis, sem.at[0])]
-    for n in range(2):
-        source = basis_in.at[pl.ds(pl.multiple_of(scalars[2 + n], half), half), :]
-        copies.append(pltpu.make_async_copy(source, left.at[pl.ds(n * half, half), :], sem.at[1 + n]))
+def more_planes_kernel(scalars, basis_in, *refs, depth):
+    out_refs = refs[:PARTS]
+    basis, left, coef, rows, sem = refs[PARTS:]
+    size = out_refs[0].shape[0]
+    copies = [pltpu.make_async_copy(basis_in, basis, sem.at[PARTS])]
+    for n in range(PARTS):
+        source = basis_in.at[pl.ds(pl.multiple_of(scalars[2 + n], size), size), :]
+        copies.append(pltpu.make_async_copy(source, left.at[pl.ds(n * size, size), :], sem.at[n]))
     for copy in copies:
         copy.start()
     coefficients_into(coef, scalars[0], scalars[1], depth, 64)
     for copy in copies:
         copy.wait()
-    transform_into(out_ref, left, coef, rows, basis)
-
-
-def more_planes(scalars, basis, depth, count):
+    transform_into(out_refs, left, coef, rows, basis)
+
+
+def more_planes(scalars, basis, depth, size):
     return pl.pallas_call(
-        functools.partial(more_planes_kernel, depth=depth, count=count),
+        functools.partial(more_planes_kernel, depth=depth),
         in_specs=[pl.BlockSpec(memory_space=pltpu.SMEM), pl.BlockSpec(memory_space=pl.ANY)],
-        out_specs=pl.BlockSpec(memory_space=pltpu.VMEM),
-        out_shape=jax.ShapeDtypeStruct((count, LEN_Y), jnp.bfloat16),
+        out_specs=[pl.BlockSpec(memory_space=pltpu.VMEM)] * PARTS,
+        out_shape=[jax.ShapeDtypeStruct((size, LEN_Y), jnp.bfloat16)] * PARTS,
         scratch_shapes=[
             pltpu.VMEM((LEN_X, LEN_X), jnp.bfloat16),
-            pltpu.VMEM((count, LEN_X), jnp.bfloat16),
+            pltpu.VMEM((PARTS * size, LEN_X), jnp.bfloat16),
             pltpu.VMEM((LEN_X, LEN_Y), jnp.bfloat16),
-            pltpu.VMEM((count, LEN_Y), jnp.bfloat16),
-            pltpu.SemaphoreType.DMA((3,)),
+            pltpu.VMEM((PARTS * size, LEN_Y), jnp.bfloat16),
+            pltpu.SemaphoreType.DMA((PARTS + 1,)),
         ],
         compiler_params=pltpu.CompilerParams(vmem_limit_bytes=VMEM_LIMIT),
+        cost_estimate=pl.CostEstimate(flops=20_000_000_000, transcendentals=0, bytes_accessed=8_000_000),
         name="more_planes",
     )(scalars, basis)
 
@@ -341,38 +349,40 @@
         out_specs=pl.BlockSpec((TILE, depth, LEN_Y), lambda i: (i, 0, 0)),
         out_shape=jax.ShapeDtypeStruct((count, depth, LEN_Y), jnp.bfloat16),
         compiler_params=pltpu.CompilerParams(vmem_limit_bytes=VMEM_LIMIT),
+        cost_estimate=pl.CostEstimate(flops=1_300_000_000, transcendentals=0, bytes_accessed=10_000_000),
         name="turn",
     )(matrix, forcing)
 
 
-def perm_kernel(matrix, a_ref, b_ref, c_ref, out_ref):
-    field = None
-    start = 0
-    for ref in (a_ref, b_ref, c_ref):
-        size = ref.shape[0] * TILE
-        part = jnp.dot(
-            matrix[:, start : start + size],
-            ref[...].reshape(size, LEN_Y),
-            preferred_element_type=jnp.float32,
-        )
-        field = part if field is None else field + part
-        start += size
+def perm_kernel(matrix, *refs):
+    out_ref = refs[-1]
+    a_ref = refs[0]
+    split = a_ref.shape[0] * TILE
+    field = jnp.dot(
+        matrix[:, :split], a_ref[...].reshape(split, LEN_Y), preferred_element_type=jnp.float32
+    )
+    rest = jnp.concatenate([ref[...] for ref in refs[1:-1]], axis=0)
+    field = field + jnp.dot(matrix[:, split:], rest, preferred_element_type=jnp.float32)
     out_ref[...] = jnp.exp(1.5 * jnp.tanh(2.0 * field)).astype(jnp.bfloat16).reshape(out_ref.shape)
 
 
-def permeability(matrix, parts):
-    count = parts[0].shape[1]
-    depth = sum(part.shape[0] for part in parts)
+def permeability(matrix, block, planes):
+    modes, count, _ = block.shape
+    depth = modes + len(planes)
     return pl.pallas_call(
         perm_kernel,
         grid=(count // TILE,),
-        in_specs=[pl.BlockSpec(matrix.shape, lambda i: (0, 0))]
-        + [pl.BlockSpec((part.shape[0], TILE, LEN_Y), lambda i: (0, i, 0)) for part in parts],
+        in_specs=[
+            pl.BlockSpec(matrix.shape, lambda i: (0, 0)),
+            pl.BlockSpec((modes, TILE, LEN_Y), lambda i: (0, i, 0)),
+        ]
+        + [pl.BlockSpec((TILE, LEN_Y), lambda i: (i, 0)) for _ in planes],
         out_specs=pl.BlockSpec((TILE, depth, LEN_Y), lambda i: (i, 0, 0)),
         out_shape=jax.ShapeDtypeStruct((count, depth, LEN_Y), jnp.bfloat16),
         compiler_params=pltpu.CompilerParams(vmem_limit_bytes=VMEM_LIMIT),
+        cost_estimate=pl.CostEstimate(flops=1_300_000_000, transcendentals=0, bytes_accessed=10_000_000),
         name="permeability",
-    )(matrix, *parts)
+    )(matrix, block, *planes)
 
 
 def chebyshev():
@@ -545,46 +555,39 @@
 def body(stream_index, forcing):
     depth, count, _ = forcing.shape
     index = lax.axis_index("wide")
-    core = index % 2
-    side = index // 2 % 2
-    far = index // 4 % 2
-    color = side ^ far
+    core = index & 1
+    color = (index >> 1 ^ index >> 2) & 1
     key = scramble(stream_index[0] ^ 1540483477)
-    own = index // 2 * 2 * count
     shared = DEPTH // 2 + 4 * color + 2 * core
 
-    first, basis = first_planes(
-        jnp.stack([key, index % 8, index // 8 * 8 * count]).astype(jnp.int32), depth, 8 * count
-    )
+    scalars = jnp.stack([key, index & 7, (index >> 3) * (8 * count)]).astype(jnp.int32)
+    first, basis = first_planes(scalars, depth, 8 * count)
     groups = [list(range(8)), list(range(8, 16))]
-    part_a = lax.all_to_all(
+    block = lax.all_to_all(
         first.reshape(8, count, LEN_Y), "wide", 0, 0, axis_index_groups=groups, tiled=True
     )
 
-    def pairwise(mode, other, basis, groups):
-        low = jnp.minimum(own, other)
-        high = jnp.maximum(own, other)
-        out = more_planes(jnp.stack([key, mode, low, high]).astype(jnp.int32), basis, depth, 4 * count)
-        part = lax.all_to_all(
-            out.reshape(4, count, LEN_Y), "wide", 0, 0, axis_index_groups=groups, tiled=True
-        )
-        return part
-
-    far_groups = [[s, s + 1, s + 4, s + 5] for s in (0, 2, 8, 10)]
-    side_groups = [[s, s + 1, s + 2, s + 3] for s in (0, 4, 8, 12)]
-    part_b = pairwise(shared, (index ^ 4) // 2 * 2 * count, basis, far_groups)
-    part_c = pairwise(shared + 1, (index ^ 2) // 2 * 2 * count, basis, side_groups)
-    slot = jnp.arange(4, dtype=jnp.int32)
-    modes_b = DEPTH // 2 + 4 * (slot // 2 ^ side) + 2 * (slot % 2)
-    modes_c = DEPTH // 2 + 4 * (slot // 2 ^ far) + 2 * (slot % 2) + 1
-    modes = jnp.concatenate([jnp.arange(8, dtype=jnp.int32), modes_b, modes_c])
-
+    def pairwise(mode, bit):
+        flips = (0, 1, bit, bit ^ 1)
+        scalars = jnp.stack([key, mode] + [(index ^ flip) * count for flip in flips]).astype(jnp.int32)
+        out = more_planes(scalars, basis, depth, count)
+        return [out[0]] + [
+            lax.ppermute(piece, "wide", [(i, i ^ flip) for i in range(WIDE)])
+            for piece, flip in zip(out[1:], flips[1:])
+        ]
+
+    planes = pairwise(shared, 4) + pairwise(shared + 1, 2)
+    half = DEPTH // 2
+    shared_modes = jnp.stack(
+        [half + 4 * (color ^ b) + 2 * (core ^ c) + a for a in (0, 1) for b in (0, 1) for c in (0, 1)]
+    )
+    modes = jnp.concatenate([jnp.arange(half, dtype=jnp.int32), shared_modes])
     swap = swap_matrix(depth)
     f_parts = edges(turn(swap, forcing))
     basis_z = basis_columns(modes, depth)
     eye = jnp.eye(TILE, dtype=jnp.bfloat16)
     mixing = (eye[:, None, None, :] * basis_z[None, :, :, None]).reshape(TILE * depth, depth * TILE)
-    k_parts = edges(permeability(mixing, [part_a, part_b, part_c]))
+    k_parts = edges(permeability(mixing, block, planes))
     flags = jnp.stack([index > 0, index < WIDE - 1]).astype(jnp.int32)
     return solve(flags, swap, f_parts, k_parts)
 

time: 220 us -> 191 us (0.87)
  blocking collectives: 20.2 us -> 0 us
  waiting for transfers between devices: 17.2 us -> 7.2 us
    all_to_all x1 -> x0, blocking collectives: 20.2 us -> none  [pairwise(): lax.all_to_all(out.reshape(4, count, LEN_Y), 'wide', 0, 0, axis_index_gro...]
    all_to_all x1, waiting for transfers between devices: 12.9 us -> 0.01 us  [body(): lax.all_to_all(first.reshape(8, count, LEN_Y), 'wide', 0, 0, axis_index_g...]
    ppermute x0 -> x6, starting transfers between devices: none -> 4.51 us  [pairwise(): lax.ppermute(piece, 'wide', [(i, i ^ flip) for i in range(WIDE)])]
    all_to_all x1 -> x0, starting transfers between devices: 3.54 us -> none  [pairwise(): lax.all_to_all(out.reshape(4, count, LEN_Y), 'wide', 0, 0, axis_index_gro...]
    ppermute x0 -> x6, waiting for transfers between devices: none -> 2.92 us  [pairwise(): lax.ppermute(piece, 'wide', [(i, i ^ flip) for i in range(WIDE)])]
  transfers between devices with their start and end apart: 6 -> 11, of which waited for: 2 -> 2; matrix products, arithmetic and copies ran while one was open for 3% -> 4% of each run, Pallas kernels for 16% -> 29%
where the time goes in v2:
time: 191 us; the launch traced here: 189 us
  Pallas kernels  153 us (80%)
  starting transfers between devices  18 us (9%)
  local copies, waits for them, and re-layouts  7.24 us (4%)
  waiting for transfers between devices  7.2 us (4%)
  other arithmetic  2.53 us (1%)
    pallas_call x1, Pallas kernels, solve(): pl.pallas_call(solve_kernel, in_specs=[pl.BlockSpec(memory_space=pltpu.SM...  70.4 us
    pallas_call x2, Pallas kernels, more_planes(): pl.pallas_call(functools.partial(more_planes_kernel, depth=depth), in_spe...  39.9 us
    pallas_call x1, Pallas kernels, first_planes(): pl.pallas_call(functools.partial(first_planes_kernel, depth=depth, count=...  27.7 us
    pallas_call x1, Pallas kernels, permeability(): pl.pallas_call(perm_kernel, grid=(count // TILE,), in_specs=[pl.BlockSpec...  8.04 us
    pallas_call x1, Pallas kernels, turn(): pl.pallas_call(turn_kernel, grid=(count // TILE,), in_specs=[pl.BlockSpec...  7.01 us
    ppermute x2, starting transfers between devices, edges(): high = lax.ppermute(block[:HALO], 'wide', backward)  5.35 us
    ppermute x6, starting transfers between devices, pairwise(): lax.ppermute(piece, 'wide', [(i, i ^ flip) for i in range(WIDE)])  4.51 us
    ppermute x2, starting transfers between devices, edges(): low = lax.ppermute(block[-HALO:], 'wide', forward)  4.3 us
  transfers between devices with their start and end apart: 11, of which 2 were waited for; matrix products, arithmetic and copies ran while one was open for 4% of the time, Pallas kernels for 29%

profile of v2, /device:TPU:18, one launch (start us, length us, event | category | flops | bytes accessed | tf_op | source)
XLA Modules:
  0.0 188.9 jit_solution(3102603814961943320)
XLA Ops:
  1.3 27.7 %first_planes.1 = (bf16[768,1536]{1,0:T(8,128)(2,1)}, bf16[1536,1536]{1,0:T(8,128)(2,1)}) custom-call(s32[3]{0:T(128)} %pad_add_fusion.scalars), custom_call_target="tpu_custom_call" | custom-call | flops 24999999488 | bytes 8000000 | tf_op jit(solution)/shard_map/first_planes/pallas_call | solution.py:268
  29.0 3.8 %all-to-all-start = ((bf16[8,96,1536]{2,1,0:T(8,128)(2,1)}), bf16[8,96,1536]{2,1,0:T(8,128)(2,1)S(1)}, u32[]{:S(2)}, u32[]{:S(2)}) async-start(bf16[8,96,1536]{2,1,0:T(8,128)(2,1)} %bitcast.23), calls=%async_computation | async-start | bytes 4718592 | tf_op jit(solution)/shard_map/all_to_all | solution.py:566
  32.8 0.7 stack.73.scalars
  33.5 19.9 %more_planes.3 = (bf16[96,1536]{1,0:T(8,128)(2,1)}, bf16[96,1536]{1,0:T(8,128)(2,1)}, bf16[96,1536]{1,0:T(8,128)(2,1)}, bf16[96,1536]{1,0:T(8,128)(2,1)}) custom-call(s32[6]{0:T(128)} %stack.73.scalars, bf16[1536,1536]{1,0:T(8,128)(2,1)} %get-tuple-element.16.basis_in), custom_call_target="tpu_custom_call" | custom-call | flops 20000000000 | bytes 8000000 | tf_op jit(solution)/shard_map/more_planes/pallas_call | solution.py:309
  53.9 1.7 collective-permute-start.6
  55.6 0.7 stack.70.scalars
  56.3 20.0 %more_planes.2 = (bf16[96,1536]{1,0:T(8,128)(2,1)}, bf16[96,1536]{1,0:T(8,128)(2,1)}, bf16[96,1536]{1,0:T(8,128)(2,1)}, bf16[96,1536]{1,0:T(8,128)(2,1)}) custom-call(s32[6]{0:T(128)} %stack.70.scalars, bf16[1536,1536]{1,0:T(8,128)(2,1)} %get-tuple-element.16.basis_in), custom_call_target="tpu_custom_call" | custom-call | flops 20000000000 | bytes 8000000 | tf_op jit(solution)/shard_map/more_planes/pallas_call | solution.py:309
  76.8 1.7 collective-permute-start.3
  78.9 1.7 mul.138.matrix
  80.6 0.9 fusion.matrix.swap
  81.5 7.0 %turn.1.f_in = bf16[96,16,1536]{2,1,0:T(8,128)(2,1)} custom-call(bf16[256,256]{1,0:T(8,128)(2,1)} %fusion.matrix.swap, bf16[16,96,1536]{2,1,0:T(8,128)(2,1)} %in_ref.1), custom_call_target="tpu_custom_call" | custom-call | flops 1300000000 | bytes 10000000 | tf_op jit(solution)/shard_map/turn/pallas_call | solution.py:342
  88.6 1.0 fusion.11
  89.6 3.4 %collective-permute-start.1 = (bf16[3,16,1536]{2,1,0:T(8,128)(2,1)S(1)}, bf16[3,16,1536]{2,1,0:T(8,128)(2,1)S(1)}, u32[]{:S(2)}, u32[]{:S(2)}) collective-permute-start(bf16[3,16,1536]{2,1,0:T(8,128)(2,1)S(1)} %get-tuple-element.27), channel_id=1, source_target_pairs={{1,0},{2,1},{3,2},{4,3},{5,4},{6,5},{7,6},{8,7},{9,8},{10,9},{11,1... | collective-permute-start | bytes 442376 | tf_op jit(solution)/shard_map/ppermute | solution.py:543
  93.0 1.9 %collective-permute-start = (bf16[3,16,1536]{2,1,0:T(8,128)(2,1)S(1)}, bf16[3,16,1536]{2,1,0:T(8,128)(2,1)S(1)}, u32[]{:S(2)}, u32[]{:S(2)}) collective-permute-start(bf16[3,16,1536]{2,1,0:T(8,128)(2,1)S(1)} %get-tuple-element.28), channel_id=1, source_target_pairs={{0,1},{1,2},{2,3},{3,4},{4,5},{5,6},{6,7},{7,8},{8,9},{9,10},{10,1... | collective-permute-start | bytes 442376 | tf_op jit(solution)/shard_map/ppermute | solution.py:542
  95.0 2.9 %collective-permute-done.4.refs_4_ = bf16[96,1536]{1,0:T(8,128)(2,1)S(1)} collective-permute-done((bf16[96,1536]{1,0:T(8,128)(2,1)S(1)}, bf16[96,1536]{1,0:T(8,128)(2,1)S(1)}, u32[]{:S(2)}, u32[]{:S(2)}) %collective-permute-start.4) | collective-permute-done | bytes 294944 | tf_op jit(solution)/shard_map/ppermute | solution.py:575
  97.9 0.7 copy-done.1
  98.6 0.8 copy-done
  99.4 8.0 %permeability.1.k_in = bf16[96,16,1536]{2,1,0:T(8,128)(2,1)} custom-call(bf16[256,256]{1,0:T(8,128)(2,1)} %mul.138.matrix, bf16[8,96,1536]{2,1,0:T(8,128)(2,1)} %copy-done, bf16[96,1536]{1,0:T(8,128)(2,1)} %get-tuple-element.17.refs_1_, bf16[96,1536]{1,0:T(8,128)(2,1)} %collective-permute-done.2.refs_2_, bf16[96,1536]{1,0:T(8,128)(2,1)} %collective-permute-done.3.refs_3_, ...), custom_call_target="tpu_custom_call" | custom-call | flops 1300000000 | bytes 10000000 | tf_op jit(solution)/shard_map/permeability/pallas_call | solution.py:372
  107.4 1.0 fusion.10
  108.4 1.9 %collective-permute-start.9 = (bf16[3,16,1536]{2,1,0:T(8,128)(2,1)S(1)}, bf16[3,16,1536]{2,1,0:T(8,128)(2,1)S(1)}, u32[]{:S(2)}, u32[]{:S(2)}) collective-permute-start(bf16[3,16,1536]{2,1,0:T(8,128)(2,1)S(1)} %get-tuple-element.25), channel_id=1, source_target_pairs={{1,0},{2,1},{3,2},{4,3},{5,4},{6,5},{7,6},{8,7},{9,8},{10,9},{11,1... | collective-permute-start | bytes 442376 | tf_op jit(solution)/shard_map/ppermute | solution.py:543
  110.4 2.4 %collective-permute-start.8 = (bf16[3,16,1536]{2,1,0:T(8,128)(2,1)S(1)}, bf16[3,16,1536]{2,1,0:T(8,128)(2,1)S(1)}, u32[]{:S(2)}, u32[]{:S(2)}) collective-permute-start(bf16[3,16,1536]{2,1,0:T(8,128)(2,1)S(1)} %get-tuple-element.26), channel_id=1, source_target_pairs={{0,1},{1,2},{2,3},{3,4},{4,5},{5,6},{6,7},{7,8},{8,9},{9,10},{10,1... | collective-permute-start | bytes 442376 | tf_op jit(solution)/shard_map/ppermute | solution.py:542
  112.8 0.7 add_convert_fusion.flags
  113.5 4.3 %collective-permute-done.8.k_low = bf16[3,16,1536]{2,1,0:T(8,128)(2,1)S(1)} collective-permute-done((bf16[3,16,1536]{2,1,0:T(8,128)(2,1)S(1)}, bf16[3,16,1536]{2,1,0:T(8,128)(2,1)S(1)}, u32[]{:S(2)}, u32[]{:S(2)}) %collective-permute-start.8) | collective-permute-done | bytes 147488 | tf_op jit(solution)/shard_map/ppermute | solution.py:542
  118.4 70.4 %solve.1 = bf16[16,96,1536]{2,1,0:T(8,128)(2,1)} custom-call(s32[2]{0:T(128)} %add_convert_fusion.flags, bf16[256,256]{1,0:T(8,128)(2,1)} %fusion.matrix.swap, bf16[96,16,1536]{2,1,0:T(8,128)(2,1)} %turn.1.f_in, bf16[3,16,1536]{2,1,0:T(8,128)(2,1)} %copy-done.3, bf16[3,16,1536]{2,1,0:T(8,128)(2,1)} %copy-done.2, bf16[96,16,1536]{2,1,0:T(8,128)(2,1)} %permeability.1.k_in, ...), custom_call_target="tpu_custom_call" | custom-call | tf_op jit(solution)/shard_map/solve/pallas_call | solution.py:518
  (36 shorter events, 2.9 us)
Async XLA Ops:
  29.0 68.9 %all-to-all-start = ((bf16[8,96,1536]{2,1,0:T(8,128)(2,1)}), bf16[8,96,1536]{2,1,0:T(8,128)(2,1)S(1)}, u32[]{:S(2)}, u32[]{:S(2)}) async-start(bf16[8,96,1536]{2,1,0:T(8,128)(2,1)} %bitcast.23), calls=%async_computation | async-start | bytes 4718592 | tf_op jit(solution)/shard_map/all_to_all | solution.py:566
  53.4 35.1 %collective-permute-start.5 = (bf16[96,1536]{1,0:T(8,128)(2,1)}, bf16[96,1536]{1,0:T(8,128)(2,1)}, u32[]{:S(2)}, u32[]{:S(2)}) collective-permute-start(bf16[96,1536]{1,0:T(8,128)(2,1)} %get-tuple-element.22), channel_id=1, source_target_pairs={{0,1},{1,0},{2,3},{3,2},{4,5},{5,4},{6,7},{7,6},{8,9},{9,8},{10,11... | collective-permute-start | bytes 884744 | tf_op jit(solution)/shard_map/ppermute | solution.py:575
  53.9 35.7 %collective-permute-start.6 = (bf16[96,1536]{1,0:T(8,128)(2,1)}, bf16[96,1536]{1,0:T(8,128)(2,1)}, u32[]{:S(2)}, u32[]{:S(2)}) collective-permute-start(bf16[96,1536]{1,0:T(8,128)(2,1)} %get-tuple-element.23), channel_id=1, source_target_pairs={{0,2},{1,3},{2,0},{3,1},{4,6},{5,7},{6,4},{7,5},{8,10},{9,11},{10,... | collective-permute-start | bytes 884744 | tf_op jit(solution)/shard_map/ppermute | solution.py:575
  55.6 37.4 %collective-permute-start.7 = (bf16[96,1536]{1,0:T(8,128)(2,1)}, bf16[96,1536]{1,0:T(8,128)(2,1)}, u32[]{:S(2)}, u32[]{:S(2)}) collective-permute-start(bf16[96,1536]{1,0:T(8,128)(2,1)} %get-tuple-element.24), channel_id=1, source_target_pairs={{0,3},{1,2},{2,1},{3,0},{4,7},{5,6},{6,5},{7,4},{8,11},{9,10},{10,... | collective-permute-start | bytes 884744 | tf_op jit(solution)/shard_map/ppermute | solution.py:575
  76.3 18.7 %collective-permute-start.2 = (bf16[96,1536]{1,0:T(8,128)(2,1)}, bf16[96,1536]{1,0:T(8,128)(2,1)}, u32[]{:S(2)}, u32[]{:S(2)}) collective-permute-start(bf16[96,1536]{1,0:T(8,128)(2,1)} %get-tuple-element.18), channel_id=1, source_target_pairs={{0,1},{1,0},{2,3},{3,2},{4,5},{5,4},{6,7},{7,6},{8,9},{9,8},{10,11... | collective-permute-start | bytes 884744 | tf_op jit(solution)/shard_map/ppermute | solution.py:575
  76.8 18.2 %collective-permute-start.3 = (bf16[96,1536]{1,0:T(8,128)(2,1)}, bf16[96,1536]{1,0:T(8,128)(2,1)}, u32[]{:S(2)}, u32[]{:S(2)}) collective-permute-start(bf16[96,1536]{1,0:T(8,128)(2,1)} %get-tuple-element.19), channel_id=1, source_target_pairs={{0,4},{1,5},{2,6},{3,7},{4,0},{5,1},{6,2},{7,3},{8,12},{9,13},{10,... | collective-permute-start | bytes 884744 | tf_op jit(solution)/shard_map/ppermute | solution.py:575
  81.5 7.0 %copy-start.6 = (bf16[96,1536]{1,0:T(8,128)(2,1)S(1)}, bf16[96,1536]{1,0:T(8,128)(2,1)}, u32[]{:S(2)}) copy-start(bf16[96,1536]{1,0:T(8,128)(2,1)} %get-tuple-element.20) | copy-start | bytes 884740
  88.5 9.4 %collective-permute-start.4 = (bf16[96,1536]{1,0:T(8,128)(2,1)S(1)}, bf16[96,1536]{1,0:T(8,128)(2,1)S(1)}, u32[]{:S(2)}, u32[]{:S(2)}) collective-permute-start(bf16[96,1536]{1,0:T(8,128)(2,1)S(1)} %copy-done.6), channel_id=1, source_target_pairs={{0,5},{1,4},{2,7},{3,6},{4,1},{5,0},{6,3},{7,2},{8,13},{9,12},{10,... | collective-permute-start | bytes 884744 | tf_op jit(solution)/shard_map/ppermute | solution.py:575
  89.6 23.8 %collective-permute-start.1 = (bf16[3,16,1536]{2,1,0:T(8,128)(2,1)S(1)}, bf16[3,16,1536]{2,1,0:T(8,128)(2,1)S(1)}, u32[]{:S(2)}, u32[]{:S(2)}) collective-permute-start(bf16[3,16,1536]{2,1,0:T(8,128)(2,1)S(1)} %get-tuple-element.27), channel_id=1, source_target_pairs={{1,0},{2,1},{3,2},{4,3},{5,4},{6,5},{7,6},{8,7},{9,8},{10,9},{11,1... | collective-permute-start | bytes 442376 | tf_op jit(solution)/shard_map/ppermute | solution.py:543
  93.0 20.4 %collective-permute-start = (bf16[3,16,1536]{2,1,0:T(8,128)(2,1)S(1)}, bf16[3,16,1536]{2,1,0:T(8,128)(2,1)S(1)}, u32[]{:S(2)}, u32[]{:S(2)}) collective-permute-start(bf16[3,16,1536]{2,1,0:T(8,128)(2,1)S(1)} %get-tuple-element.28), channel_id=1, source_target_pairs={{0,1},{1,2},{2,3},{3,4},{4,5},{5,6},{6,7},{7,8},{8,9},{9,10},{10,1... | collective-permute-start | bytes 442376 | tf_op jit(solution)/shard_map/ppermute | solution.py:542
  97.9 0.7 copy-start.1
  97.9 1.5 copy-start
  108.4 5.0 %collective-permute-start.9 = (bf16[3,16,1536]{2,1,0:T(8,128)(2,1)S(1)}, bf16[3,16,1536]{2,1,0:T(8,128)(2,1)S(1)}, u32[]{:S(2)}, u32[]{:S(2)}) collective-permute-start(bf16[3,16,1536]{2,1,0:T(8,128)(2,1)S(1)} %get-tuple-element.25), channel_id=1, source_target_pairs={{1,0},{2,1},{3,2},{4,3},{5,4},{6,5},{7,6},{8,7},{9,8},{10,9},{11,1... | collective-permute-start | bytes 442376 | tf_op jit(solution)/shard_map/ppermute | solution.py:543
  110.4 7.4 %collective-permute-start.8 = (bf16[3,16,1536]{2,1,0:T(8,128)(2,1)S(1)}, bf16[3,16,1536]{2,1,0:T(8,128)(2,1)S(1)}, u32[]{:S(2)}, u32[]{:S(2)}) collective-permute-start(bf16[3,16,1536]{2,1,0:T(8,128)(2,1)S(1)} %get-tuple-element.26), channel_id=1, source_target_pairs={{0,1},{1,2},{2,3},{3,4},{4,5},{5,6},{6,7},{7,8},{8,9},{9,10},{10,1... | collective-permute-start | bytes 442376 | tf_op jit(solution)/shard_map/ppermute | solution.py:542
  113.4 4.3 %copy-start.2 = (bf16[3,16,1536]{2,1,0:T(8,128)(2,1)}, bf16[3,16,1536]{2,1,0:T(8,128)(2,1)S(1)}, u32[]{:S(2)}) copy-start(bf16[3,16,1536]{2,1,0:T(8,128)(2,1)S(1)} %collective-permute-done.1.f_high) | copy-start | bytes 442372
  113.4 4.3 %copy-start.3 = (bf16[3,16,1536]{2,1,0:T(8,128)(2,1)}, bf16[3,16,1536]{2,1,0:T(8,128)(2,1)S(1)}, u32[]{:S(2)}) copy-start(bf16[3,16,1536]{2,1,0:T(8,128)(2,1)S(1)} %collective-permute-done.f_low) | copy-start | bytes 442372
  113.5 4.3 %copy-start.4 = (bf16[3,16,1536]{2,1,0:T(8,128)(2,1)}, bf16[3,16,1536]{2,1,0:T(8,128)(2,1)S(1)}, u32[]{:S(2)}) copy-start(bf16[3,16,1536]{2,1,0:T(8,128)(2,1)S(1)} %collective-permute-done.9.k_high) | copy-start | bytes 442372
  117.8 0.7 copy-start.5

commit v3 on v2

--- a/solution.py
+++ b/solution.py
@@ -132,7 +132,7 @@
 HALO = ITERS - 1
 PARTS = 4
 TILE = 16
-VMEM_LIMIT = 58 << 20
+VMEM_LIMIT = 60 << 20
 THETA = 27.9
 DELTA = 26.1
 SIN_PI = (
@@ -324,36 +324,6 @@
     )(scalars, basis)
 
 
-def swap_matrix(depth):
-    size = depth * TILE
-    row = lax.broadcasted_iota(jnp.int32, (size, size), 0)
-    col = lax.broadcasted_iota(jnp.int32, (size, size), 1)
-    return (col == (row % depth) * TILE + row // depth).astype(jnp.bfloat16)
-
-
-def turn_kernel(matrix, in_ref, out_ref):
-    tile = in_ref[...].reshape(matrix.shape[1], LEN_Y)
-    turned = jnp.dot(matrix[...], tile, preferred_element_type=jnp.float32)
-    out_ref[...] = turned.astype(jnp.bfloat16).reshape(out_ref.shape)
-
-
-def turn(matrix, forcing):
-    depth, count, _ = forcing.shape
-    return pl.pallas_call(
-        turn_kernel,
-        grid=(count // TILE,),
-        in_specs=[
-            pl.BlockSpec(matrix.shape, lambda i: (0, 0)),
-            pl.BlockSpec((depth, TILE, LEN_Y), lambda i: (0, i, 0)),
-        ],
-        out_specs=pl.BlockSpec((TILE, depth, LEN_Y), lambda i: (i, 0, 0)),
-        out_shape=jax.ShapeDtypeStruct((count, depth, LEN_Y), jnp.bfloat16),
-        compiler_params=pltpu.CompilerParams(vmem_limit_bytes=VMEM_LIMIT),
-        cost_estimate=pl.CostEstimate(flops=1_300_000_000, transcendentals=0, bytes_accessed=10_000_000),
-        name="turn",
-    )(matrix, forcing)
-
-
 def perm_kernel(matrix, *refs):
     out_ref = refs[-1]
     a_ref = refs[0]
@@ -377,8 +347,8 @@
             pl.BlockSpec((modes, TILE, LEN_Y), lambda i: (0, i, 0)),
         ]
         + [pl.BlockSpec((TILE, LEN_Y), lambda i: (i, 0)) for _ in planes],
-        out_specs=pl.BlockSpec((TILE, depth, LEN_Y), lambda i: (i, 0, 0)),
-        out_shape=jax.ShapeDtypeStruct((count, depth, LEN_Y), jnp.bfloat16),
+        out_specs=pl.BlockSpec((depth, TILE, LEN_Y), lambda i: (0, i, 0)),
+        out_shape=jax.ShapeDtypeStruct((depth, count, LEN_Y), jnp.bfloat16),
         compiler_params=pltpu.CompilerParams(vmem_limit_bytes=VMEM_LIMIT),
         cost_estimate=pl.CostEstimate(flops=1_300_000_000, transcendentals=0, bytes_accessed=10_000_000),
         name="permeability",
@@ -397,151 +367,215 @@
 
 
 def solve_kernel(
-    flags, swap, f_in, f_low, f_high, k_in, k_low, k_high, out_ref, f, kb, kh, pa, pb, tile, flux, sem
+    flags, f_in, f_edge, k_in, k_edge, out_ref, kh, ky, pa, pb, pc, stage, turned, mask, fx, fz, sem_in, sem_out
 ):
-    count, depth, _ = f_in.shape
-    total = count + 2 * HALO
-    copies = []
-    for n, (low, mid, high, target) in enumerate(((f_low, f_in, f_high, f), (k_low, k_in, k_high, kb))):
-        for m, (ref, start) in enumerate(((low, 0), (mid, HALO), (high, HALO + count))):
-            copies.append(
-                pltpu.make_async_copy(ref, target.at[pl.ds(start, ref.shape[0])], sem.at[3 * n + m])
+    depth, count, _ = f_in.shape
+    padded = kh.shape[1]
+    tiles = padded // 8
+    rows_in = count + TILE
+    blocks = LEN_Y // 128
+    chunk = stage.shape[2]
+    chunks = depth // chunk
+
+    def copies(c, slot):
+        found = []
+        for n, (mid, edge) in enumerate(((f_in, f_edge), (k_in, k_edge))):
+            at = pl.ds(c * chunk, chunk)
+            found.append(
+                pltpu.make_async_copy(mid.at[at], stage.at[slot, n, :, pl.ds(0, count), :], sem_in.at[slot, n, 0])
             )
-    for copy in copies:
+            found.append(
+                pltpu.make_async_copy(edge.at[at], stage.at[slot, n, :, pl.ds(count, TILE), :], sem_in.at[slot, n, 1])
+            )
+        return found
+
+    for copy in copies(0, 0):
         copy.start()
-    for copy in copies:
-        copy.wait()
-
-    def prepare(e, carry):
-        kh[e] = 0.5 * kb[e].astype(jnp.float32)
-        pa[e] = f[e].astype(jnp.float32) * (1.0 / THETA)
-        return carry
-
-    lax.fori_loop(0, total, prepare, 0)
-    lane = lax.broadcasted_iota(jnp.int32, (depth, 128), 1)
-    level = lax.broadcasted_iota(jnp.int32, (depth, 128), 0)
-    blocks = LEN_Y // 128
+
+    def padded_row(index):
+        return (index & 7) * tiles + (index >> 3)
+
+    row = padded_row(lax.broadcasted_iota(jnp.int32, (padded, rows_in), 0))
+    source = jnp.where(row < HALO, row + count, jnp.where(row < HALO + count, row - HALO, row))
+    spread = (lax.broadcasted_iota(jnp.int32, (padded, rows_in), 1) == source).astype(jnp.bfloat16)
+    place = padded_row(lax.broadcasted_iota(jnp.int32, (count, padded), 1))
+    gather = (lax.broadcasted_iota(jnp.int32, (count, padded), 0) + HALO == place).astype(jnp.bfloat16)
+    row = padded_row(lax.broadcasted_iota(jnp.int32, (padded, 128), 0))
+    outside = ((row < HALO) & (flags[0] == 0)) | ((row >= HALO + count) & (flags[1] == 0))
+    mask[...] = jnp.where(outside, 0.0, 1.0)
+    lane = lax.broadcasted_iota(jnp.int32, (8, 128), 1)
 
     def cols(j):
         return slice(j * 128, (j + 1) * 128)
 
-    def up(value):
-        return jnp.where(level == depth - 1, 0.0, pltpu.roll(value, depth - 1, 0))
-
-    def iteration(first, last, src, store):
+    for c in range(chunks):
+        slot = c % 2
+        if c + 1 < chunks:
+            for copy in copies(c + 1, 1 - slot):
+                copy.start()
+        for copy in copies(c, slot):
+            copy.wait()
+        for m in range(chunk):
+            z = c * chunk + m
+            for n in range(0, LEN_Y, 256):
+                pa[z, :, n : n + 256] = jnp.dot(
+                    spread, stage[slot, 0, m, :, n : n + 256], preferred_element_type=jnp.float32
+                ) * (1.0 / THETA)
+                kh[z, :, n : n + 256] = 0.5 * jnp.dot(
+                    spread, stage[slot, 1, m, :, n : n + 256], preferred_element_type=jnp.float32
+                )
+
+    def faces(n, carry):
+        z = n // tiles
+        at = pl.ds(pl.multiple_of((n - z * tiles) * 8, 8), 8)
+        here = kh[z, at, cols(0)]
+        turn = pltpu.roll(here, 127, 1)
         for j in range(blocks):
-            k_here = kh[first - 1, :, cols(j)]
-            k_next = kh[first, :, cols(j)]
-            flux[:, cols(j)] = (k_here + k_next) * (src[first - 1, :, cols(j)] - src[first, :, cols(j)])
-
-        def row(e, carry):
-            p = src[e, :, cols(0)]
-            k = kh[e, :, cols(0)]
-            p_turn = pltpu.roll(p, 127, 1)
-            k_turn = pltpu.roll(k, 127, 1)
-            before = None
+            if j + 1 < blocks:
+                after = kh[z, at, cols(j + 1)]
+                after_turn = pltpu.roll(after, 127, 1)
+            else:
+                after, after_turn = None, 0.0
+            ky[z, at, cols(j)] = here + jnp.where(lane == 127, after_turn, turn)
+            here, turn = after, after_turn
+        return carry
+
+    lax.fori_loop(0, depth * tiles, faces, 0)
+
+    def wrapped(value):
+        return pltpu.roll(value, 7, 0)
+
+    def sweep(src, store):
+        last = slice(padded - 8, padded)
+
+        def begin(z, carry):
             for j in range(blocks):
-                if j + 1 < blocks:
-                    p_after = src[e, :, cols(j + 1)]
-                    k_after = kh[e, :, cols(j + 1)]
-                    p_after_turn = pltpu.roll(p_after, 127, 1)
-                    k_after_turn = pltpu.roll(k_after, 127, 1)
-                else:
-                    p_after = k_after = None
-                    p_after_turn = k_after_turn = 0.0
-                p_right = jnp.where(lane == 127, p_after_turn, p_turn)
-                k_right = jnp.where(lane == 127, k_after_turn, k_turn)
-                flow_y = (k + k_right) * (p - p_right)
-                flow_turn = pltpu.roll(flow_y, 1, 1)
-                left = jnp.where(lane == 0, -k * p if before is None else before, flow_turn)
-                before = flow_turn
-                flow_z = (k + up(k)) * (p - up(p))
-                under = jnp.where(level == 0, -k * p, pltpu.roll(flow_z, 1, 0))
-                flow_x = (k + kh[e + 1, :, cols(j)]) * (p - src[e + 1, :, cols(j)])
-                out = (flow_x - flux[:, cols(j)]) + (flow_y - left) + (flow_z - under)
-                flux[:, cols(j)] = flow_x
-                store(e, j, p, out)
-                p, k, p_turn, k_turn = p_after, k_after, p_after_turn, k_after_turn
+                flow = (kh[z, last, cols(j)] + wrapped(kh[z, 0:8, cols(j)])) * (
+                    src[z, last, cols(j)] - wrapped(src[z, 0:8, cols(j)])
+                )
+                fx[z, :, cols(j)] = pltpu.roll(flow, 1, 0)
             return carry
 
-        return row
-
-    def clear(ref, first, last):
-        @pl.when(flags[0] == 0)
-        def _():
-            for e in range(first, HALO):
-                ref[e] = jnp.zeros(ref.shape[1:], ref.dtype)
-
-        @pl.when(flags[1] == 0)
-        def _():
-            for e in range(HALO + count, last):
-                ref[e] = jnp.zeros(ref.shape[1:], ref.dtype)
+        lax.fori_loop(0, depth, begin, 0)
+
+        def tile(i, wrap):
+            at = pl.ds(i * 8, 8) if wrap else pl.ds(pl.multiple_of(i * 8, 8), 8)
+            factor = mask[at, :]
+            for j in range(blocks):
+                fz[:, cols(j)] = -kh[0, at, cols(j)] * src[0, at, cols(j)]
+
+            def level(z, top):
+                def beside(ref, j):
+                    if wrap:
+                        return wrapped(ref[z, 0:8, cols(j)])
+                    return ref[z, pl.ds(pl.multiple_of(i * 8 + 8, 8), 8), cols(j)]
+
+                p = src[z, at, cols(0)]
+                p_turn = pltpu.roll(p, 127, 1)
+                before = None
+                for j in range(blocks):
+                    k = kh[z, at, cols(j)]
+                    if j + 1 < blocks:
+                        p_after = src[z, at, cols(j + 1)]
+                        p_after_turn = pltpu.roll(p_after, 127, 1)
+                    else:
+                        p_after, p_after_turn = None, 0.0
+                    flow_y = ky[z, at, cols(j)] * (p - jnp.where(lane == 127, p_after_turn, p_turn))
+                    flow_turn = pltpu.roll(flow_y, 1, 1)
+                    left = jnp.where(lane == 0, -k * p if before is None else before, flow_turn)
+                    before = flow_turn
+                    if top:
+                        flow_z = k * p
+                    else:
+                        flow_z = (k + kh[z + 1, at, cols(j)]) * (p - src[z + 1, at, cols(j)])
+                    flow_x = (k + beside(kh, j)) * (p - beside(src, j))
+                    out = (flow_x - fx[z, :, cols(j)]) + (flow_y - left) + (flow_z - fz[:, cols(j)])
+                    if not wrap:
+                        fx[z, :, cols(j)] = flow_x
+                    if not top:
+                        fz[:, cols(j)] = flow_z
+                    store((z, at, cols(j)), p, out, factor)
+                    p, p_turn = p_after, p_after_turn
+
+            def lower(z, carry):
+                level(z, False)
+                return carry
+
+            lax.fori_loop(0, depth - 1, lower, 0)
+            level(depth - 1, True)
+
+        def inner(i, carry):
+            tile(i, False)
+            return carry
+
+        lax.fori_loop(0, tiles - 1, inner, 0)
+        tile(tiles - 1, True)
 
     (a1, b1), (a2, b2), (a3, b3) = chebyshev()
 
-    def store_one(e, j, p, out):
-        pb[e, :, cols(j)] = (1.0 + a1 + b1 * THETA) * p - b1 * out
-
-    def store_two(e, j, p, out):
-        old = f[e, :, cols(j)].astype(jnp.float32)
-        pa[e, :, cols(j)] = (1.0 + a2) * p + (b2 - a2 / THETA) * old - b2 * out
-
-    lax.fori_loop(1, total - 1, iteration(1, total - 1, pa, store_one), 0)
-    clear(pb, 1, total - 1)
-    lax.fori_loop(2, total - 2, iteration(2, total - 2, pb, store_two), 0)
-    clear(pa, 2, total - 2)
-
-    def store_three(e, j, p, out):
-        source = f[e, :, cols(j)].astype(jnp.float32)
-        value = (1.0 + a3) * p - a3 * pb[e, :, cols(j)] + b3 * (source - out)
-        tile[(e - HALO) % TILE, :, cols(j)] = value.astype(jnp.bfloat16)
-
-    row = iteration(HALO, total - HALO, pa, store_three)
-
-    def strip(t, carry):
-        lax.fori_loop(HALO + t * TILE, HALO + (t + 1) * TILE, row, 0)
-        turned = jnp.dot(
-            swap[...], tile[...].reshape(TILE * depth, LEN_Y), preferred_element_type=jnp.float32
-        )
-        out_ref[:, pl.ds(pl.multiple_of(t * TILE, TILE), TILE), :] = turned.astype(jnp.bfloat16).reshape(
-            depth, TILE, LEN_Y
-        )
-        return carry
-
-    lax.fori_loop(0, count // TILE, strip, 0)
-
-
-def solve(flags, swap, f_parts, k_parts):
-    count, depth, _ = f_parts[0].shape
-    total = count + 2 * HALO
+    def store_one(at, p, out, factor):
+        pb[at] = (1.0 + a1 + b1 * THETA) * p - (b1 * factor) * out
+
+    def store_two(at, p, out, factor):
+        pc[at] = (1.0 + a2) * p + (b2 * THETA - a2) * pa[at] - (b2 * factor) * out
+
+    def store_three(at, p, out, factor):
+        pb[at] = ((1.0 + a3) * p - b3 * out) + (b3 * THETA * pa[at] - a3 * pb[at])
+
+    sweep(pa, store_one)
+    sweep(pb, store_two)
+    sweep(pc, store_three)
+
+    def leave(z):
+        return pltpu.make_async_copy(turned.at[z % 2], out_ref.at[z], sem_out.at[z % 2])
+
+    for z in range(depth):
+        if z > 1:
+            leave(z - 2).wait()
+        for n in range(0, LEN_Y, 256):
+            turned[z % 2, :, n : n + 256] = jnp.dot(
+                gather, pb[z, :, n : n + 256].astype(jnp.bfloat16), preferred_element_type=jnp.float32
+            ).astype(jnp.bfloat16)
+        leave(z).start()
+    for z in (depth - 2, depth - 1):
+        leave(z).wait()
+
+
+def solve(flags, f, f_edge, k, k_edge):
+    depth, count, _ = f.shape
+    padded = -(-(count + 2 * HALO) // 8) * 8
     anywhere = pl.BlockSpec(memory_space=pl.ANY)
+    whole = pltpu.VMEM((depth, padded, LEN_Y), jnp.float32)
     return pl.pallas_call(
         solve_kernel,
-        in_specs=[pl.BlockSpec(memory_space=pltpu.SMEM), pl.BlockSpec(memory_space=pltpu.VMEM)]
-        + [anywhere] * 6,
-        out_specs=pl.BlockSpec(memory_space=pltpu.VMEM),
+        in_specs=[pl.BlockSpec(memory_space=pltpu.SMEM)] + [anywhere] * 4,
+        out_specs=anywhere,
         out_shape=jax.ShapeDtypeStruct((depth, count, LEN_Y), jnp.bfloat16),
         scratch_shapes=[
-            pltpu.VMEM((total, depth, LEN_Y), jnp.bfloat16),
-            pltpu.VMEM((total, depth, LEN_Y), jnp.bfloat16),
-            pltpu.VMEM((total, depth, LEN_Y), jnp.float32),
-            pltpu.VMEM((total, depth, LEN_Y), jnp.float32),
-            pltpu.VMEM((total, depth, LEN_Y), jnp.float32),
-            pltpu.VMEM((TILE, depth, LEN_Y), jnp.bfloat16),
-            pltpu.VMEM((depth, LEN_Y), jnp.float32),
-            pltpu.SemaphoreType.DMA((6,)),
+            whole,
+            whole,
+            whole,
+            whole,
+            whole,
+            pltpu.VMEM((2, 2, 2, count + TILE, LEN_Y), jnp.bfloat16),
+            pltpu.VMEM((2, count, LEN_Y), jnp.bfloat16),
+            pltpu.VMEM((padded, 128), jnp.float32),
+            pltpu.VMEM((depth, 8, LEN_Y), jnp.float32),
+            pltpu.VMEM((8, LEN_Y), jnp.float32),
+            pltpu.SemaphoreType.DMA((2, 2, 2)),
+            pltpu.SemaphoreType.DMA((2,)),
         ],
         compiler_params=pltpu.CompilerParams(vmem_limit_bytes=VMEM_LIMIT),
         name="solve",
-    )(flags, swap, *f_parts, *k_parts)
+    )(flags, f, f_edge, k, k_edge)
 
 
 def edges(block):
     forward = [(i, i + 1) for i in range(WIDE - 1)]
     backward = [(target, source) for source, target in forward]
-    low = lax.ppermute(block[-HALO:], "wide", forward)
-    high = lax.ppermute(block[:HALO], "wide", backward)
-    return block, low, high
+    low = lax.ppermute(block[:, -HALO:], "wide", forward)
+    high = lax.ppermute(block[:, :HALO], "wide", backward)
+    return jnp.pad(jnp.concatenate([low, high], axis=1), ((0, 0), (0, TILE - 2 * HALO), (0, 0)))
 
 
 def basis_columns(modes, length):
@@ -582,14 +616,12 @@
         [half + 4 * (color ^ b) + 2 * (core ^ c) + a for a in (0, 1) for b in (0, 1) for c in (0, 1)]
     )
     modes = jnp.concatenate([jnp.arange(half, dtype=jnp.int32), shared_modes])
-    swap = swap_matrix(depth)
-    f_parts = edges(turn(swap, forcing))
     basis_z = basis_columns(modes, depth)
     eye = jnp.eye(TILE, dtype=jnp.bfloat16)
-    mixing = (eye[:, None, None, :] * basis_z[None, :, :, None]).reshape(TILE * depth, depth * TILE)
-    k_parts = edges(permeability(mixing, block, planes))
+    mixing = (basis_z[:, None, :, None] * eye[None, :, None, :]).reshape(depth * TILE, depth * TILE)
+    perm = permeability(mixing, block, planes)
     flags = jnp.stack([index > 0, index < WIDE - 1]).astype(jnp.int32)
-    return solve(flags, swap, f_parts, k_parts)
+    return solve(flags, forcing, edges(forcing), perm, edges(perm))
 
 
 def solution(mesh):

time: 191 us -> 251 us (1.31)
  Pallas kernels: 153 us -> 210 us
  starting transfers between devices: 18 us -> 21.4 us
  waiting for transfers between devices: 7.2 us -> 4.43 us
    pallas_call x1, Pallas kernels: 70.4 us -> 134 us  [solve(): pl.pallas_call(solve_kernel, in_specs=[pl.BlockSpec(memory_space=pltpu.SM...]
    pallas_call x1 -> x0, Pallas kernels: 7.01 us -> none  [turn(): pl.pallas_call(turn_kernel, grid=(count // TILE,), in_specs=[pl.BlockSpec...]
    ppermute x4, starting transfers between devices: 9.65 us -> 13.1 us  [the longest x2 8.36 us: edges(): high = lax.ppermute(block[:, :HALO], 'wide', backward)]
    ppermute x4, waiting for transfers between devices: 4.28 us -> 1.73 us  [the longest x2 1.73 us: edges(): high = lax.ppermute(block[:, :HALO], 'wide', backward)]
  transfers between devices with their start and end apart: 11 -> 11, of which waited for: 2 -> 2; matrix products, arithmetic and copies ran while one was open for 4% -> 3% of each run, Pallas kernels for 29% -> 19%
where the time goes in v3:
time: 251 us; the launch traced here: 248 us
  Pallas kernels  210 us (84%)
  starting transfers between devices  21.4 us (9%)
  local copies, waits for them, and re-layouts  7.03 us (3%)
  waiting for transfers between devices  4.43 us (2%)
  other arithmetic  3.92 us (2%)
    pallas_call x1, Pallas kernels, solve(): pl.pallas_call(solve_kernel, in_specs=[pl.BlockSpec(memory_space=pltpu.SM...  134 us
    pallas_call x2, Pallas kernels, more_planes(): pl.pallas_call(functools.partial(more_planes_kernel, depth=depth), in_spe...  39.8 us
    pallas_call x1, Pallas kernels, first_planes(): pl.pallas_call(functools.partial(first_planes_kernel, depth=depth, count=...  27.7 us
    ppermute x2, starting transfers between devices, edges(): high = lax.ppermute(block[:, :HALO], 'wide', backward)  8.36 us
    pallas_call x1, Pallas kernels, permeability(): pl.pallas_call(perm_kernel, grid=(count // TILE,), in_specs=[pl.BlockSpec...  8.02 us
  transfers between devices with their start and end apart: 11, of which 2 were waited for; matrix products, arithmetic and copies ran while one was open for 3% of the time, Pallas kernels for 19%

profile of v3, /device:TPU:18, one launch (start us, length us, event | category | flops | bytes accessed | tf_op | source)
XLA Modules:
  0.0 247.6 jit_solution(14649949949139483591)
XLA Ops:
  0.7 0.6 pad_add_fusion.scalars
  1.3 27.7 %first_planes.1 = (bf16[768,1536]{1,0:T(8,128)(2,1)}, bf16[1536,1536]{1,0:T(8,128)(2,1)}) custom-call(s32[3]{0:T(128)} %pad_add_fusion.scalars), custom_call_target="tpu_custom_call" | custom-call | flops 24999999488 | bytes 8000000 | tf_op jit(solution)/shard_map/first_planes/pallas_call | solution.py:268
  29.0 3.8 %all-to-all-start = ((bf16[8,96,1536]{2,1,0:T(8,128)(2,1)}), bf16[8,96,1536]{2,1,0:T(8,128)(2,1)S(1)}, u32[]{:S(2)}, u32[]{:S(2)}) async-start(bf16[8,96,1536]{2,1,0:T(8,128)(2,1)} %bitcast.23), calls=%async_computation | async-start | bytes 4718592 | tf_op jit(solution)/shard_map/all_to_all | solution.py:600
  32.8 0.6 stack.73.scalars
  33.5 19.9 %more_planes.3 = (bf16[96,1536]{1,0:T(8,128)(2,1)}, bf16[96,1536]{1,0:T(8,128)(2,1)}, bf16[96,1536]{1,0:T(8,128)(2,1)}, bf16[96,1536]{1,0:T(8,128)(2,1)}) custom-call(s32[6]{0:T(128)} %stack.73.scalars, bf16[1536,1536]{1,0:T(8,128)(2,1)} %get-tuple-element.16.basis_in), custom_call_target="tpu_custom_call" | custom-call | flops 20000000000 | bytes 8000000 | tf_op jit(solution)/shard_map/more_planes/pallas_call | solution.py:309
  53.9 1.7 collective-permute-start.6
  55.6 0.6 stack.70.scalars
  56.2 19.9 %more_planes.2 = (bf16[96,1536]{1,0:T(8,128)(2,1)}, bf16[96,1536]{1,0:T(8,128)(2,1)}, bf16[96,1536]{1,0:T(8,128)(2,1)}, bf16[96,1536]{1,0:T(8,128)(2,1)}) custom-call(s32[6]{0:T(128)} %stack.70.scalars, bf16[1536,1536]{1,0:T(8,128)(2,1)} %get-tuple-element.16.basis_in), custom_call_target="tpu_custom_call" | custom-call | flops 20000000000 | bytes 8000000 | tf_op jit(solution)/shard_map/more_planes/pallas_call | solution.py:309
  76.6 1.7 collective-permute-start.3
  78.7 1.6 mul.128.matrix
  81.0 1.3 fusion.14
  82.3 2.4 collective-permute-start
  84.7 4.1 %collective-permute-start.1 = (bf16[16,3,1536]{2,1,0:T(4,128)(2,1)S(1)}, bf16[16,3,1536]{2,1,0:T(4,128)(2,1)S(1)}, u32[]{:S(2)}, u32[]{:S(2)}) collective-permute-start(bf16[16,3,1536]{2,1,0:T(4,128)(2,1)S(1)} %get-tuple-element.28), channel_id=1, source_target_pairs={{1,0},{2,1},{3,2},{4,3},{5,4},{6,5},{7,6},{8,7},{9,8},{10,9},{11,1... | collective-permute-start | bytes 442376 | tf_op jit(solution)/shard_map/ppermute | solution.py:577
  88.8 2.7 %collective-permute-done.4.refs_4_ = bf16[96,1536]{1,0:T(8,128)(2,1)S(1)} collective-permute-done((bf16[96,1536]{1,0:T(8,128)(2,1)}, bf16[96,1536]{1,0:T(8,128)(2,1)S(1)}, u32[]{:S(2)}, u32[]{:S(2)}) %collective-permute-start.4) | collective-permute-done | bytes 294944 | tf_op jit(solution)/shard_map/ppermute | solution.py:609
  91.5 0.7 copy-done.1
  92.2 0.8 copy-done
  93.0 8.0 %permeability.1.k_in = bf16[16,96,1536]{2,1,0:T(8,128)(2,1)} custom-call(bf16[256,256]{1,0:T(8,128)(2,1)} %mul.128.matrix, bf16[8,96,1536]{2,1,0:T(8,128)(2,1)} %copy-done, bf16[96,1536]{1,0:T(8,128)(2,1)} %get-tuple-element.17.refs_1_, bf16[96,1536]{1,0:T(8,128)(2,1)} %collective-permute-done.2.refs_2_, bf16[96,1536]{1,0:T(8,128)(2,1)} %collective-permute-done.3.refs_3_, ...), custom_call_target="tpu_custom_call" | custom-call | flops 1300000000 | bytes 10000000 | tf_op jit(solution)/shard_map/permeability/pallas_call | solution.py:342
  101.0 1.3 fusion.13
  102.3 2.4 collective-permute-start.8
  104.7 4.3 %collective-permute-start.9 = (bf16[16,3,1536]{2,1,0:T(4,128)(2,1)S(1)}, bf16[16,3,1536]{2,1,0:T(4,128)(2,1)S(1)}, u32[]{:S(2)}, u32[]{:S(2)}) collective-permute-start(bf16[16,3,1536]{2,1,0:T(4,128)(2,1)S(1)} %get-tuple-element.26), channel_id=1, source_target_pairs={{1,0},{2,1},{3,2},{4,3},{5,4},{6,5},{7,6},{8,7},{9,8},{10,9},{11,1... | collective-permute-start | bytes 442376 | tf_op jit(solution)/shard_map/ppermute | solution.py:577
  109.0 1.2 fusion.4.f_edge
  110.2 1.7 collective-permute-done.9
  111.9 1.2 fusion.5.k_edge
  113.1 134.4 %solve.1 = bf16[16,96,1536]{2,1,0:T(8,128)(2,1)} custom-call(s32[2]{0:T(128)} %add_convert_fusion.flags, bf16[16,96,1536]{2,1,0:T(8,128)(2,1)} %f_in.1, bf16[16,16,1536]{2,1,0:T(8,128)(2,1)} %fusion.4.f_edge, bf16[16,96,1536]{2,1,0:T(8,128)(2,1)} %permeability.1.k_in, bf16[16,16,1536]{2,1,0:T(8,128)(2,1)} %fusion.5.k_edge), custom_call_target="tpu_custom_call" | custom-call | tf_op jit(solution)/shard_map/solve/pallas_call | solution.py:549
  (23 shorter events, 2.1 us)
Async XLA Ops:
  29.0 62.5 %all-to-all-start = ((bf16[8,96,1536]{2,1,0:T(8,128)(2,1)}), bf16[8,96,1536]{2,1,0:T(8,128)(2,1)S(1)}, u32[]{:S(2)}, u32[]{:S(2)}) async-start(bf16[8,96,1536]{2,1,0:T(8,128)(2,1)} %bitcast.23), calls=%async_computation | async-start | bytes 4718592 | tf_op jit(solution)/shard_map/all_to_all | solution.py:600
  53.4 27.6 %collective-permute-start.5 = (bf16[96,1536]{1,0:T(8,128)(2,1)}, bf16[96,1536]{1,0:T(8,128)(2,1)}, u32[]{:S(2)}, u32[]{:S(2)}) collective-permute-start(bf16[96,1536]{1,0:T(8,128)(2,1)} %get-tuple-element.22), channel_id=1, source_target_pairs={{0,1},{1,0},{2,3},{3,2},{4,5},{5,4},{6,7},{7,6},{8,9},{9,8},{10,11... | collective-permute-start | bytes 884744 | tf_op jit(solution)/shard_map/ppermute | solution.py:609
  53.9 28.3 %collective-permute-start.6 = (bf16[96,1536]{1,0:T(8,128)(2,1)}, bf16[96,1536]{1,0:T(8,128)(2,1)}, u32[]{:S(2)}, u32[]{:S(2)}) collective-permute-start(bf16[96,1536]{1,0:T(8,128)(2,1)} %get-tuple-element.23), channel_id=1, source_target_pairs={{0,2},{1,3},{2,0},{3,1},{4,6},{5,7},{6,4},{7,5},{8,10},{9,11},{10,... | collective-permute-start | bytes 884744 | tf_op jit(solution)/shard_map/ppermute | solution.py:609
  55.6 29.0 %collective-permute-start.7 = (bf16[96,1536]{1,0:T(8,128)(2,1)}, bf16[96,1536]{1,0:T(8,128)(2,1)}, u32[]{:S(2)}, u32[]{:S(2)}) collective-permute-start(bf16[96,1536]{1,0:T(8,128)(2,1)} %get-tuple-element.24), channel_id=1, source_target_pairs={{0,3},{1,2},{2,1},{3,0},{4,7},{5,6},{6,5},{7,4},{8,11},{9,10},{10,... | collective-permute-start | bytes 884744 | tf_op jit(solution)/shard_map/ppermute | solution.py:609
  76.1 12.6 %collective-permute-start.2 = (bf16[96,1536]{1,0:T(8,128)(2,1)}, bf16[96,1536]{1,0:T(8,128)(2,1)}, u32[]{:S(2)}, u32[]{:S(2)}) collective-permute-start(bf16[96,1536]{1,0:T(8,128)(2,1)} %get-tuple-element.18), channel_id=1, source_target_pairs={{0,1},{1,0},{2,3},{3,2},{4,5},{5,4},{6,7},{7,6},{8,9},{9,8},{10,11... | collective-permute-start | bytes 884744 | tf_op jit(solution)/shard_map/ppermute | solution.py:609
  76.6 12.1 %collective-permute-start.3 = (bf16[96,1536]{1,0:T(8,128)(2,1)}, bf16[96,1536]{1,0:T(8,128)(2,1)}, u32[]{:S(2)}, u32[]{:S(2)}) collective-permute-start(bf16[96,1536]{1,0:T(8,128)(2,1)} %get-tuple-element.19), channel_id=1, source_target_pairs={{0,4},{1,5},{2,6},{3,7},{4,0},{5,1},{6,2},{7,3},{8,12},{9,13},{10,... | collective-permute-start | bytes 884744 | tf_op jit(solution)/shard_map/ppermute | solution.py:609
  81.0 10.5 %collective-permute-start.4 = (bf16[96,1536]{1,0:T(8,128)(2,1)}, bf16[96,1536]{1,0:T(8,128)(2,1)S(1)}, u32[]{:S(2)}, u32[]{:S(2)}) collective-permute-start(bf16[96,1536]{1,0:T(8,128)(2,1)} %get-tuple-element.20), channel_id=1, source_target_pairs={{0,5},{1,4},{2,7},{3,6},{4,1},{5,0},{6,3},{7,2},{8,13},{9,12},{10,... | collective-permute-start | bytes 884744 | tf_op jit(solution)/shard_map/ppermute | solution.py:609
  82.3 26.7 %collective-permute-start = (bf16[16,3,1536]{2,1,0:T(4,128)(2,1)S(1)}, bf16[16,3,1536]{2,1,0:T(4,128)(2,1)S(1)}, u32[]{:S(2)}, u32[]{:S(2)}) collective-permute-start(bf16[16,3,1536]{2,1,0:T(4,128)(2,1)S(1)} %get-tuple-element.27), channel_id=1, source_target_pairs={{0,1},{1,2},{2,3},{3,4},{4,5},{5,6},{6,7},{7,8},{8,9},{9,10},{10,1... | collective-permute-start | bytes 442376 | tf_op jit(solution)/shard_map/ppermute | solution.py:576
  84.7 24.3 %collective-permute-start.1 = (bf16[16,3,1536]{2,1,0:T(4,128)(2,1)S(1)}, bf16[16,3,1536]{2,1,0:T(4,128)(2,1)S(1)}, u32[]{:S(2)}, u32[]{:S(2)}) collective-permute-start(bf16[16,3,1536]{2,1,0:T(4,128)(2,1)S(1)} %get-tuple-element.28), channel_id=1, source_target_pairs={{1,0},{2,1},{3,2},{4,3},{5,4},{6,5},{7,6},{8,7},{9,8},{10,9},{11,1... | collective-permute-start | bytes 442376 | tf_op jit(solution)/shard_map/ppermute | solution.py:577
  91.5 0.7 copy-start.1
  91.5 1.5 copy-start
  102.3 7.9 %collective-permute-start.8 = (bf16[16,3,1536]{2,1,0:T(4,128)(2,1)S(1)}, bf16[16,3,1536]{2,1,0:T(4,128)(2,1)S(1)}, u32[]{:S(2)}, u32[]{:S(2)}) collective-permute-start(bf16[16,3,1536]{2,1,0:T(4,128)(2,1)S(1)} %get-tuple-element.25), channel_id=1, source_target_pairs={{0,1},{1,2},{2,3},{3,4},{4,5},{5,6},{6,7},{7,8},{8,9},{9,10},{10,1... | collective-permute-start | bytes 442376 | tf_op jit(solution)/shard_map/ppermute | solution.py:576
  104.7 7.2 %collective-permute-start.9 = (bf16[16,3,1536]{2,1,0:T(4,128)(2,1)S(1)}, bf16[16,3,1536]{2,1,0:T(4,128)(2,1)S(1)}, u32[]{:S(2)}, u32[]{:S(2)}) collective-permute-start(bf16[16,3,1536]{2,1,0:T(4,128)(2,1)S(1)} %get-tuple-element.26), channel_id=1, source_target_pairs={{1,0},{2,1},{3,2},{4,3},{5,4},{6,5},{7,6},{8,7},{9,8},{10,9},{11,1... | collective-permute-start | bytes 442376 | tf_op jit(solution)/shard_map/ppermute | solution.py:577
